TPU v7x, 32 devices: a whole 2x2x4 slice. The times are simulated.
32 devices in a mesh: ctx: 16 (over z, x, core), fsdp: 2 (over y).
Axes of the slice: x: 2, y: 2, z: 4, core: 2. Of those that a mesh axis runs over, the one named last changes fastest.
Arguments:
- inputs: float32 [2, 2048, 640], P('fsdp', 'ctx'), may hold values from -6 to 6
- cotangent: float32 [2, 2048, 640], P('fsdp', 'ctx'), may hold values from -6 to 6
- positions: int32 [2, 2048], P('fsdp', 'ctx'), may hold values from 0 to 4094, as said below
- block_map: int32 [32], replicated, may hold values from 0 to 31, as said below
- matrices: float32 [5570560], P(('ctx', 'fsdp'))
- gain_offsets: float32 [3072], P(('ctx', 'fsdp')), as said below
- first_moment: float32 [5570560], P(('ctx', 'fsdp')), may hold values from -40 to 40
- second_moment: float32 [5570560], P(('ctx', 'fsdp')), may hold values from 102.4 to 1638.4
- gain_first: float32 [3072], P(('ctx', 'fsdp')), may hold values from -40 to 40
- gain_second: float32 [3072], P(('ctx', 'fsdp')), may hold values from 102.4 to 1638.4
Outputs:
- outputs: float32 [2, 2048, 640], P('fsdp', 'ctx')
- input_grad: float32 [2, 2048, 640], P('fsdp', 'ctx')
- matrix_grad: float32 [5570560], P(('ctx', 'fsdp'))
- gain_grad: float32 [3072], P(('ctx', 'fsdp'))
- new_matrices: float32 [5570560], P(('ctx', 'fsdp'))
- new_gains: float32 [3072], P(('ctx', 'fsdp'))
- new_first: float32 [5570560], P(('ctx', 'fsdp'))
- new_second: float32 [5570560], P(('ctx', 'fsdp'))
- new_gain_first: float32 [3072], P(('ctx', 'fsdp'))
- new_gain_second: float32 [3072], P(('ctx', 'fsdp'))
Inputs may be any that keep to these rules, and one draw needn't show every extreme that they name: block_map is a permutation; storage slots 2 c and 2 c + 1 hold blocks b and 31 - b for some b. Read in causal order, each sequence's positions start at 0 and rise by 1 to 3 from one token to the next; the rises after tokens 2 i and 2 i + 1 sum to 4, so the last token's position is 4094. `gain_offsets`: every entry lies between -0.1 and 0.3.
All inputs are finite; a program needn't handle non-finite values.
Results may differ from a plain program's by a relative error of at most 0.024.
Values may be sent and summed in bfloat16 or wider, within the bound.
A program may use at most 192 MiB of HBM per device.

v0:
```python
import jax
import jax.numpy as jnp
from jax import lax
from jax.sharding import PartitionSpec as P

D = 640
HEADS = 4
HD = 256
FF = 2048
BLK = 64
STEP = 3


NORM_EPS = 1e-06
ROPE_BASE = 1000000.0
LEARN_RATE = 0.03
BETA_ONE = 0.9
BETA_TWO = 0.95
ADAM_EPS = 1e-08
DECAY_RATE = 0.1


def rms_apply(values, offset):
    scale_rows = lax.rsqrt(jnp.mean(values * values, axis=-1, keepdims=True) + NORM_EPS)
    return values * scale_rows * (1.0 + offset)


def norm_back(values, offset, upstream):
    _, pullback = jax.vjp(rms_apply, values, offset)
    return pullback(upstream)


def gated_unit(gate_values, up_values):
    return jax.nn.gelu(gate_values, approximate=True) * up_values


def rope_tables(token_pos):
    half_width = HD // 2
    exponents = jnp.arange(half_width, dtype=jnp.float32) * (2.0 / HD)
    frequency = jnp.power(jnp.float32(ROPE_BASE), -exponents)
    angles = token_pos.astype(jnp.float32)[:, None] * frequency[None, :]
    cosine_table = jnp.cos(angles)
    sine_table = jnp.sin(angles)
    return (
        jnp.concatenate([cosine_table, cosine_table], axis=-1),
        jnp.concatenate([sine_table, sine_table], axis=-1),
    )


def rotate(values, cosine_table, sine_table):
    half_width = values.shape[-1] // 2
    first_half = values[..., :half_width]
    second_half = values[..., half_width:]
    turned = jnp.concatenate([-second_half, first_half], axis=-1)
    return values * cosine_table + turned * sine_table


def rotate_back(upstream, cosine_table, sine_table):
    half_width = upstream.shape[-1] // 2
    weighted = upstream * sine_table
    turned = jnp.concatenate([weighted[..., half_width:], -weighted[..., :half_width]], axis=-1)
    return upstream * cosine_table + turned


def split_weights(flat_values):
    width_qkv = HEADS * HD + 2 * HD
    first_end = D * width_qkv
    second_end = first_end + HEADS * HD * D
    third_end = second_end + 2 * D * FF
    return (
        flat_values[:first_end].reshape(D, width_qkv),
        flat_values[first_end:second_end].reshape(HEADS * HD, D),
        flat_values[second_end:third_end].reshape(D, 2 * FF),
        flat_values[third_end:].reshape(FF, D),
    )


def split_gains(flat_values):
    return (
        flat_values[:D],
        flat_values[D : D + HD],
        flat_values[D + HD : D + 2 * HD],
        flat_values[D + 2 * HD : 2 * D + 2 * HD],
        flat_values[2 * D + 2 * HD : 3 * D + 2 * HD],
        flat_values[3 * D + 2 * HD :],
    )


def adamw_update(weights, first_state, second_state, gradient):
    new_first = BETA_ONE * first_state + (1.0 - BETA_ONE) * gradient
    new_second = BETA_TWO * second_state + (1.0 - BETA_TWO) * gradient * gradient
    first_hat = new_first / (1.0 - BETA_ONE**STEP)
    second_hat = new_second / (1.0 - BETA_TWO**STEP)
    update = first_hat / (jnp.sqrt(second_hat) + ADAM_EPS) + DECAY_RATE * weights
    return (weights - LEARN_RATE * update, new_first, new_second)


def tile_forward(carried, query_rows, query_order, key_rows, value_rows, key_order):
    row_peak, row_total, row_accum = carried
    scores = lax.dot_general(
        key_rows, query_rows, (((1,), (1,)), ((), ())), preferred_element_type=jnp.float32
    )
    allowed = key_order[:, None] <= query_order[None, :]
    masked = jnp.where(allowed, scores, -jnp.inf)
    new_peak = jnp.maximum(row_peak, jnp.max(masked, axis=0))
    weights = jnp.exp(masked - new_peak[None, :])
    rescale = jnp.exp(row_peak - new_peak)
    new_total = row_total * rescale + jnp.sum(weights, axis=0)
    weights_low = weights.astype(jnp.bfloat16)
    update = lax.dot_general(
        weights_low, value_rows, (((0,), (0,)), ((), ())), preferred_element_type=jnp.float32
    )
    return (new_peak, new_total, row_accum * rescale[:, None] + update)


def tile_backward(
    query_rows, query_order, grad_rows, log_total, delta_rows, key_rows, value_rows, key_order
):
    scores = lax.dot_general(
        key_rows, query_rows, (((1,), (1,)), ((), ())), preferred_element_type=jnp.float32
    )
    allowed = key_order[:, None] <= query_order[None, :]
    probability = jnp.where(allowed, jnp.exp(scores - log_total[None, :]), 0.0)
    probability_low = probability.astype(jnp.bfloat16)
    value_part = jnp.dot(probability_low, grad_rows, preferred_element_type=jnp.float32)
    grad_prob = lax.dot_general(
        value_rows, grad_rows, (((1,), (1,)), ((), ())), preferred_element_type=jnp.float32
    )
    grad_scores = (probability * (grad_prob - delta_rows[None, :])).astype(jnp.bfloat16)
    query_part = lax.dot_general(
        grad_scores, key_rows, (((0,), (0,)), ((), ())), preferred_element_type=jnp.float32
    )
    key_part = jnp.dot(grad_scores, query_rows, preferred_element_type=jnp.float32)
    return (query_part, jnp.concatenate([key_part, value_part], axis=1))


def add_rows(term_rows, tile_rows, first_row):
    current = lax.dynamic_slice_in_dim(term_rows, first_row, tile_rows.shape[0], 0)
    return lax.dynamic_update_slice_in_dim(term_rows, current + tile_rows, first_row, 0)


def shards(
    inputs,
    cotangent,
    positions,
    block_map,
    matrices,
    gain_offsets,
    first_moment,
    second_moment,
    gain_first,
    gain_second,
):
    gathered, gains_low = (
        lax.all_gather(matrices.astype(jnp.bfloat16), ("ctx", "fsdp"), axis=0, tiled=True),
        lax.all_gather(gain_offsets.astype(jnp.bfloat16), ("ctx", "fsdp"), axis=0, tiled=True),
    )
    w_qkv, w_out, w_gateup, w_down = split_weights(gathered)
    gain_in, gain_query, gain_key, gain_attn, gain_ffn, gain_post = split_gains(
        gains_low.astype(jnp.float32)
    )
    token_rows = inputs.shape[1]
    query_count = token_rows * HEADS
    upper_span = BLK * HEADS
    query_scale = HD ** (-0.5)
    residual_in = inputs[0]
    grad_output = cotangent[0]
    num_blocks = block_map.shape[0]
    block_ids = jnp.arange(num_blocks, dtype=jnp.int32)
    block_offsets = jnp.arange(BLK, dtype=jnp.int32)
    ctx_index = lax.axis_index("ctx")
    own_blocks = jnp.sum(
        jnp.where(
            (2 * ctx_index + jnp.arange(2, dtype=jnp.int32))[:, None] == block_ids[None, :],
            block_map[None, :],
            0,
        ),
        axis=1,
    )
    lower_block = jnp.min(own_blocks)
    upper_block = jnp.max(own_blocks)
    upper_start = jnp.where(own_blocks[1] > own_blocks[0], 1, 0) * upper_span
    token_order = (own_blocks[:, None] * BLK + block_offsets[None, :]).reshape(token_rows)
    query_order = jnp.repeat(token_order, HEADS)
    cosine_table, sine_table = rope_tables(positions[0])
    normed_in = rms_apply(residual_in, gain_in).astype(jnp.bfloat16)
    projected = jnp.dot(normed_in, w_qkv, preferred_element_type=jnp.float32)
    query_raw = projected[:, : HEADS * HD].reshape(token_rows, HEADS, HD)
    key_raw = projected[:, HEADS * HD : HEADS * HD + HD]
    value_raw = projected[:, HEADS * HD + HD :]
    query_normed = rms_apply(query_raw, gain_query)
    key_normed = rms_apply(key_raw, gain_key)
    query_rows = (
        (rotate(query_normed, cosine_table[:, None], sine_table[:, None]) * query_scale)
        .astype(jnp.bfloat16)
        .reshape(query_count, HD)
    )
    key_blocks = (
        rotate(key_normed, cosine_table, sine_table).astype(jnp.bfloat16).reshape(2, BLK, HD)
    )
    value_blocks = value_raw.astype(jnp.bfloat16).reshape(2, BLK, HD)
    upper_queries = lax.dynamic_slice_in_dim(query_rows, upper_start, upper_span, 0)
    upper_order = lax.dynamic_slice_in_dim(query_order, upper_start, upper_span, 0)

    def group_forward(carried, key_rows, value_rows, key_order, least_block):

        def group_full_rows(inner):
            return tile_forward(inner, query_rows, query_order, key_rows, value_rows, key_order)

        def group_upper_rows(inner):
            part_state = tuple(
                (lax.dynamic_slice_in_dim(member, upper_start, upper_span, 0) for member in inner)
            )
            new_state = tile_forward(
                part_state, upper_queries, upper_order, key_rows, value_rows, key_order
            )
            return tuple(
                (
                    lax.dynamic_update_slice_in_dim(member, fresh, upper_start, 0)
                    for member, fresh in zip(inner, new_state)
                )
            )

        def group_no_rows(inner):
            return inner

        branch = jnp.where(
            least_block <= lower_block, 0, jnp.where(least_block <= upper_block, 1, 2)
        )
        return lax.switch(branch, [group_full_rows, group_upper_rows, group_no_rows], carried)

    group_blocks = 16
    group_count = num_blocks // group_blocks
    group_keys = group_blocks * BLK
    group_index = jnp.arange(group_count, dtype=jnp.int32)
    init_forward = (
        jnp.full((query_count,), -jnp.inf, jnp.float32),
        jnp.zeros((query_count,), jnp.float32),
        jnp.zeros((query_count, HD), jnp.float32),
    )
    all_keys, all_values = (
        lax.all_gather(key_blocks, "ctx", axis=0, tiled=True),
        lax.all_gather(value_blocks, "ctx", axis=0, tiled=True),
    )
    inverse = jnp.sum(
        jnp.where(block_map[None, :] == block_ids[:, None], block_ids[None, :], 0), axis=1
    )
    sorted_keys = all_keys[inverse].reshape(group_count, group_keys, HD)
    sorted_values = all_values[inverse].reshape(group_count, group_keys, HD)

    def kept_forward(inner, scan_item):
        key_rows, value_rows, group_id = scan_item
        key_order = group_id * group_keys + jnp.arange(group_keys, dtype=jnp.int32)
        return (
            group_forward(inner, key_rows, value_rows, key_order, group_id * group_blocks),
            None,
        )

    forward_state, _ = lax.scan(
        kept_forward, init_forward, (sorted_keys, sorted_values, group_index)
    )
    row_peak, row_total, row_accum = forward_state
    log_total = row_peak + jnp.log(row_total)
    attn_rows = lax.optimization_barrier((row_accum / row_total[:, None]).astype(jnp.bfloat16))
    attn_flat = attn_rows.reshape(token_rows, HEADS * HD)
    branch_attn = jnp.dot(attn_flat, w_out, preferred_element_type=jnp.float32)
    after_attn = residual_in + rms_apply(branch_attn, gain_attn)
    normed_mid = rms_apply(after_attn, gain_ffn).astype(jnp.bfloat16)
    gate_up = jnp.dot(normed_mid, w_gateup, preferred_element_type=jnp.float32)
    gate_values = gate_up[:, :FF]
    up_values = gate_up[:, FF:]
    hidden = gated_unit(gate_values, up_values).astype(jnp.bfloat16)
    branch_ffn = jnp.dot(hidden, w_down, preferred_element_type=jnp.float32)
    result = after_attn + rms_apply(branch_ffn, gain_post)
    grad_branch, grad_gain_post = norm_back(branch_ffn, gain_post, grad_output)
    grad_branch_low = grad_branch.astype(jnp.bfloat16)
    grad_down = jnp.dot(hidden.T, grad_branch_low, preferred_element_type=jnp.float32)
    grad_hidden = jnp.dot(grad_branch_low, w_down.T, preferred_element_type=jnp.float32)
    _, unit_pull = jax.vjp(gated_unit, gate_values, up_values)
    grad_gate, grad_up = unit_pull(grad_hidden)
    grad_gateup_low = jnp.concatenate([grad_gate, grad_up], axis=1).astype(jnp.bfloat16)
    grad_gateup = jnp.dot(normed_mid.T, grad_gateup_low, preferred_element_type=jnp.float32)
    grad_normed_mid = jnp.dot(grad_gateup_low, w_gateup.T, preferred_element_type=jnp.float32)
    grad_mid_part, grad_gain_ffn = norm_back(after_attn, gain_ffn, grad_normed_mid)
    grad_after = grad_output + grad_mid_part
    grad_attn_branch, grad_gain_attn = norm_back(branch_attn, gain_attn, grad_after)
    grad_attn_low = grad_attn_branch.astype(jnp.bfloat16)
    grad_wout = jnp.dot(attn_flat.T, grad_attn_low, preferred_element_type=jnp.float32)
    grad_rows = lax.optimization_barrier(
        jnp.dot(grad_attn_low, w_out.T, preferred_element_type=jnp.float32).astype(jnp.bfloat16)
    ).reshape(query_count, HD)
    delta_rows = jnp.sum(grad_rows.astype(jnp.float32) * attn_rows.astype(jnp.float32), axis=1)
    upper_grads = lax.dynamic_slice_in_dim(grad_rows, upper_start, upper_span, 0)
    upper_lse = lax.dynamic_slice_in_dim(log_total, upper_start, upper_span, 0)
    upper_delta = lax.dynamic_slice_in_dim(delta_rows, upper_start, upper_span, 0)

    def tile_terms(grad_query, key_rows, value_rows, key_order, least_block):

        def tile_full_rows(inner):
            query_part, tile_rows = tile_backward(
                query_rows,
                query_order,
                grad_rows,
                log_total,
                delta_rows,
                key_rows,
                value_rows,
                key_order,
            )
            return (inner + query_part, tile_rows)

        def tile_upper_rows(inner):
            query_part, tile_rows = tile_backward(
                upper_queries,
                upper_order,
                upper_grads,
                upper_lse,
                upper_delta,
                key_rows,
                value_rows,
                key_order,
            )
            return (add_rows(inner, query_part, upper_start), tile_rows)

        def tile_no_rows(inner):
            return (inner, jnp.zeros((key_rows.shape[0], 2 * HD), jnp.float32))

        branch = jnp.where(
            least_block <= lower_block, 0, jnp.where(least_block <= upper_block, 1, 2)
        )
        return lax.switch(branch, [tile_full_rows, tile_upper_rows, tile_no_rows], grad_query)

    zero_query = jnp.zeros((query_count, HD), jnp.float32)

    def kept_backward(inner, scan_item):
        grad_query, term_rows = inner
        key_rows, value_rows, group_id = scan_item
        key_order = group_id * group_keys + jnp.arange(group_keys, dtype=jnp.int32)
        grad_query, tile_rows = tile_terms(
            grad_query, key_rows, value_rows, key_order, group_id * group_blocks
        )
        return ((grad_query, add_rows(term_rows, tile_rows, group_id * group_keys)), None)

    init_backward = (zero_query, jnp.zeros((num_blocks * BLK, 2 * HD), jnp.float32))
    backward_state, _ = lax.scan(
        kept_backward, init_backward, (sorted_keys, sorted_values, group_index)
    )
    grad_query_all, seq_terms = backward_state
    slot_terms = seq_terms.reshape(num_blocks, BLK, 2 * HD)[block_map]
    key_terms = lax.psum_scatter(slot_terms, "ctx", scatter_dimension=0, tiled=True).reshape(
        token_rows, 2 * HD
    )
    grad_key_rot = key_terms[:, :HD]
    grad_value = key_terms[:, HD:]
    grad_query_rot = grad_query_all.reshape(token_rows, HEADS, HD)
    grad_query_normed = rotate_back(
        grad_query_rot * query_scale, cosine_table[:, None], sine_table[:, None]
    )
    grad_query_raw, grad_gain_query = norm_back(query_raw, gain_query, grad_query_normed)
    grad_key_normed = rotate_back(grad_key_rot, cosine_table, sine_table)
    grad_key_raw, grad_gain_key = norm_back(key_raw, gain_key, grad_key_normed)
    grad_projected = jnp.concatenate(
        [grad_query_raw.reshape(token_rows, HEADS * HD), grad_key_raw, grad_value], axis=1
    ).astype(jnp.bfloat16)
    grad_wqkv = jnp.dot(normed_in.T, grad_projected, preferred_element_type=jnp.float32)
    grad_normed_in = jnp.dot(grad_projected, w_qkv.T, preferred_element_type=jnp.float32)
    grad_in_part, grad_gain_in = norm_back(residual_in, gain_in, grad_normed_in)
    grad_input = grad_after + grad_in_part
    local_matrix = jnp.concatenate(
        [
            grad_wqkv.reshape(-1),
            grad_wout.reshape(-1),
            grad_gateup.reshape(-1),
            grad_down.reshape(-1),
        ]
    )
    local_gain = jnp.concatenate(
        [
            grad_gain_in,
            grad_gain_query,
            grad_gain_key,
            grad_gain_attn,
            grad_gain_ffn,
            grad_gain_post,
        ]
    )
    matrix_grad, gain_grad = (
        lax.psum_scatter(local_matrix, ("ctx", "fsdp"), scatter_dimension=0, tiled=True),
        lax.psum_scatter(local_gain, ("ctx", "fsdp"), scatter_dimension=0, tiled=True),
    )
    new_matrices, new_first, new_second = adamw_update(
        matrices, first_moment, second_moment, matrix_grad
    )
    new_gains, new_gain_first, new_gain_second = adamw_update(
        gain_offsets, gain_first, gain_second, gain_grad
    )
    return (
        result[None],
        grad_input[None],
        matrix_grad,
        gain_grad,
        new_matrices,
        new_gains,
        new_first,
        new_second,
        new_gain_first,
        new_gain_second,
    )


def solution(mesh):
    return jax.shard_map(
        shards,
        mesh=mesh,
        in_specs=(
            P("fsdp", "ctx", None),
            P("fsdp", "ctx", None),
            P("fsdp", "ctx"),
            P(),
            P(("ctx", "fsdp")),
            P(("ctx", "fsdp")),
            P(("ctx", "fsdp")),
            P(("ctx", "fsdp")),
            P(("ctx", "fsdp")),
            P(("ctx", "fsdp")),
        ),
        out_specs=(
            P("fsdp", "ctx", None),
            P("fsdp", "ctx", None),
            P(("ctx", "fsdp")),
            P(("ctx", "fsdp")),
            P(("ctx", "fsdp")),
            P(("ctx", "fsdp")),
            P(("ctx", "fsdp")),
            P(("ctx", "fsdp")),
            P(("ctx", "fsdp")),
            P(("ctx", "fsdp")),
        ),
        check_vma=False,
    )
```

profile of v0, /device:TPU:0, one launch (start us, length us, event | category | flops | bytes accessed | tf_op | source)
XLA Modules:
  0.0 761.1 jit_solution(4173760600713449572)
XLA Ops:
  7.2 1.9 convert_element_type.83
  10.0 42.6 %all-reduce = bf16[3072]{0:T(1024)(128)(2,1)S(1)} all-reduce(bf16[3072]{0:T(1024)(128)(2,1)S(1)} %dynamic-update-slice), channel_id=1, replica_groups=mesh['ctx'=16,'fsdp'=2] {'ctx','fsdp'}, use_global_device_ids=true, to_apply=%add | all-reduce | flops 3072 | bytes 12288
  57.1 47.5 %all-gather.4.cloned.1.call-done = bf16[5570560]{0:T(1024)(128)(2,1)} async-done(((bf16[174080]{0:T(1024)(128)(2,1)}), bf16[5570560]{0:T(1024)(128)(2,1)}) %all-gather.4.cloned.1.call-update) | async-done | bytes 11141136 | tf_op jit(solution)/shard_map/all_gather | solution.py:155
  104.6 1.5 slice-done.2
  106.1 3.1 reshape.330
  109.3 2.1 fusion.47
  124.7 5.8 slice.163
  130.5 8.8 %slice.131 = bf16[640,4096]{1,0:T(8,128)(2,1)} reshape(bf16[2621440]{0:T(1024)(128)(2,1)} %slice.163) | data formatting | bytes 10485760 | tf_op jit(solution)/shard_map/slice | solution.py:73
  139.3 2.9 slice.166
  142.3 5.5 slice.135
  150.6 2.9 gather_fusion.1
  153.6 34.1 %all-gather.6.cloned.1.call-done = bf16[32,64,256]{2,1,0:T(8,128)(2,1)} async-done(((bf16[2,64,256]{2,1,0:T(8,128)(2,1)}), bf16[32,64,256]{2,1,0:T(8,128)(2,1)}) %all-gather.6.cloned.1.call-update) | async-done | bytes 1048592 | tf_op jit(solution)/shard_map/all_gather | solution.py:242
  187.7 2.9 gather_fusion
  190.7 22.1 %while.31 = (s32[]{:T(128)}, f32[512]{0:T(512)S(1)}, f32[512]{0:T(512)S(1)}, f32[512,256]{1,0:T(8,128)S(1)}, s32[2]{0:T(128)S(1)}, /*index=5*/s32[]{:T(128)}, s3...) while((s32[]{:T(128)}, f32[512]{0:T(512)S(1)}, ...), condition=%wide.region_15.16_spmd.clone, body=%wide.region_7.15_spmd.clone.sunk | while | flops 542902272 | bytes 10810325 | solution.py:259
  195.2 5.7 conditional.6
  199.3 1.6 convolution_add_fusion
  206.1 5.8 conditional.6
  210.0 1.9 dynamic_update_slice.12
  213.9 3.6 fusion.71
  224.1 2.4 multiply_reduce_fusion.4
  231.3 2.5 broadcast_in_dim.90.clone
  233.9 47.8 %while.32 = (s32[]{:T(128)}, f32[512,256]{1,0:T(8,128)}, f32[2048,512]{1,0:T(8,128)}, s32[2]{0:T(128)S(1)}, s32[]{:T(128)}, /*index=5*/s32[]{:T(128)}, bf16[2,10...) while((s32[]{:T(128)}, f32[512,256]{1,0:T(8,128)}, ...), condition=%wide.region_27.28_spmd.clone, body=%wide.region_23.27_spmd.clone.sunk | while | flops 1347027968 | bytes 45651260 | solution.py:345
  238.8 6.6 conditional.7
  241.5 2.3 convolution_add_fusion.2
  245.4 3.1 constant_dynamic-slice_fusion.4
  248.5 3.0 copy.64
  251.5 3.4 add.469
  254.9 1.9 copy.65
  263.2 5.5 conditional.7
  266.3 1.8 dynamic_update_slice.13
  268.7 3.1 constant_dynamic-slice_fusion.4
  271.8 3.0 copy.64
  274.8 3.4 add.469
  278.2 1.9 copy.65
  281.7 5.1 gather_fusion.2
  290.9 2.0 reshape.340
  294.4 1.7 reshape.345
  298.2 3.2 fusion.84
  301.4 7.1 reshape.347
  308.5 1.6 convolution_bitcast_fusion
  310.2 6.4 copy.61
  317.0 41.3 %reduce-scatter.2.cloned.1.call-done = f32[2,64,512]{2,1,0:T(8,128)} async-done(((f32[32,64,512]{2,1,0:T(8,128)}), f32[2,64,512]{2,1,0:T(8,128)}) %reduce-scatter.2.cloned.1.call-update) | async-done | bytes 262160 | tf_op jit(solution)/shard_map/reduce_scatter | solution.py:350
  362.7 3.2 fusion.49
  365.9 4.9 reshape.344
  370.8 23.0 %pad_maximum_fusion.2 = f32[5570560]{0:T(1024)} fusion(f32[1310720]{0:T(1024)} %reshape.347, f32[2621440]{0:T(1024)} %bitcast.130, f32[655360]{0:T(1024)S(1)} %copy-done.7, f32[983040]{0:T(1024)} %reshape.344), kind=kLoop, calls=%fused_computation.51 | loop fusion | flops 16711680 | bytes 44564480 | tf_op jit(solution)/shard_map/concatenate | solution.py:369
  396.3 41.6 %all-reduce.2 = f32[3072]{0:T(1024)S(1)} all-reduce(f32[3072]{0:T(1024)S(1)} %constant_dynamic-update-slice_fusion.1), channel_id=4, replica_groups=mesh['ctx'=16,'fsdp'=2] {'ctx','fsdp'}, use_global_device_ids=true, to_apply=%region_40.41.clone | all-reduce | flops 3072 | bytes 24576
  439.4 311.3 %all-reduce.5.cloned.1.call-done = f32[5570560]{0:T(1024)} async-done(((f32[5570560]{0:T(1024)}), f32[5570560]{0:T(1024)}) %all-reduce.5.cloned.1.call-update) | async-done | bytes 22282256
  750.7 3.4 multiply_subtract_fusion
  (341 shorter events, 76.4 us)
Async XLA Ops:
  7.2 97.4 %all-gather.4.cloned.1.call-start = ((), (), s32[]{:S(2)}) async-start(), calls=%async_computation.1 | async-start | bytes 11489280 | tf_op jit(solution)/shard_map/all_gather | solution.py:155
  9.1 141.5 %all-gather.8.cloned.1.call-start = ((), (), s32[]{:S(2)}) async-start(), calls=%async_computation.3 | async-start | bytes 1114112 | tf_op jit(solution)/shard_map/all_gather | solution.py:243
  55.8 53.4 %copy-start.61 = (f32[128]{0:T(128)}, f32[128]{0:T(128)S(1)}, u32[]{:S(2)}) copy-start(f32[128]{0:T(128)S(1)} %fusion.62) | copy-start | bytes 1540
  57.1 52.2 %copy-start.45 = (f32[640]{0:T(1024)}, f32[640]{0:T(1024)S(1)}, u32[]{:S(2)}) copy-start(f32[640]{0:T(1024)S(1)} %get-tuple-element.514) | copy-start | bytes 7684
  109.2 8.9 %copy-start.72 = (s32[32]{0:T(128)S(1)}, s32[32]{0:T(128)}, u32[]{:S(2)}) copy-start(s32[32]{0:T(128)} %param.23) | copy-start | bytes 388
  111.3 7.5 copy-start.10
  112.0 75.6 %all-gather.6.cloned.1.call-start = ((), (), s32[]{:S(2)}) async-start(), calls=%async_computation.2 | async-start | bytes 1114112 | tf_op jit(solution)/shard_map/all_gather | solution.py:242
  112.8 5.3 copy-start.52
  112.8 35.3 %copy-start.50 = (f32[256]{0:T(256)}, f32[256]{0:T(256)S(1)}, u32[]{:S(2)}) copy-start(f32[256]{0:T(256)S(1)} %get-tuple-element.515) | copy-start | bytes 3076
  113.3 4.9 copy-start.68
  113.3 4.9 copy-start.60
  114.7 243.6 %reduce-scatter.2.cloned.1.call-start = ((), (), s32[]{:S(2)}) async-start(), calls=%async_computation.4 | async-start | bytes 4456448 | tf_op jit(solution)/shard_map/reduce_scatter | solution.py:350
  119.1 28.7 %copy-start.8 = (f32[128,4,256]{2,1,0:T(4,128)}, f32[128,4,256]{2,1,0:T(4,128)S(1)}, u32[]{:S(2)}) copy-start(f32[128,4,256]{2,1,0:T(4,128)S(1)} %reshape.336) | copy-start | bytes 1572868
  122.1 8.5 %copy-start.54 = (f32[128,4]{0,1:T(4,128)}, f32[128,4]{0,1:T(4,128)S(1)}, u32[]{:S(2)}) copy-start(f32[128,4]{0,1:T(4,128)S(1)} %copy.27) | copy-start | bytes 6148
  122.2 25.6 %copy-start.29 = (f32[128,4]{1,0:T(8,128)}, f32[128,4]{1,0:T(8,128)S(1)}, u32[]{:S(2)}) copy-start(f32[128,4]{1,0:T(8,128)S(1)} %copy.28) | copy-start | bytes 6148
  213.1 4.5 copy-start.21
  213.9 12.6 %copy-start.4 = (f32[128,640]{1,0:T(8,128)}, f32[128,640]{1,0:T(8,128)S(1)}, u32[]{:S(2)}) copy-start(f32[128,640]{1,0:T(8,128)S(1)} %get-tuple-element.481) | copy-start | bytes 983044
  213.9 12.6 %copy-start.56 = (f32[128]{0:T(128)}, f32[128]{0:T(128)S(1)}, u32[]{:S(2)}) copy-start(f32[128]{0:T(128)S(1)} %fusion.65) | copy-start | bytes 1540
  228.2 5.7 copy-start.27
  234.1 3.4 copy-start.73
  234.1 4.7 copy-start
  234.1 4.7 copy-start.47
  234.1 4.7 copy-start.64
  258.5 3.4 copy-start.73
  258.5 4.7 copy-start
  258.5 4.7 copy-start.47
  258.5 4.7 copy-start.64
  286.8 463.9 %all-reduce.5.cloned.1.call-start = ((), (), s32[]{:S(2)}) async-start(), calls=%async_computation.5 | async-start | bytes 44564480
  288.8 4.2 copy-start.22
  301.4 7.1 copy-start.5
  301.4 7.1 copy-start.39
  301.4 7.1 copy-start.41
  301.4 7.1 copy-start.57
  310.1 6.4 copy-start.11
  310.2 6.4 copy-start.24
  310.2 6.4 copy-start.25
  310.2 6.4 copy-start.26
  316.6 43.6 %copy-start.36 = (f32[128,128]{1,0:T(8,128)S(1)}, f32[128,128]{1,0:T(8,128)}, u32[]{:S(2)}) copy-start(f32[128,128]{1,0:T(8,128)} %copy-done.35) | copy-start | bytes 196612
  316.6 43.6 %copy-start.53 = (f32[256]{0:T(256)S(1)}, f32[256]{0:T(256)}, u32[]{:S(2)}) copy-start(f32[256]{0:T(256)} %copy-done.52) | copy-start | bytes 3076
  316.6 46.0 %copy-start.14 = (f32[1,128,640]{2,1,0:T(8,128)S(1)}, f32[1,128,640]{2,1,0:T(8,128)}, u32[]{:S(2)}) copy-start(f32[1,128,640]{2,1,0:T(8,128)} %param.20) | copy-start | bytes 983044
  316.6 46.0 %copy-start.46 = (f32[640]{0:T(1024)S(1)}, f32[640]{0:T(1024)}, u32[]{:S(2)}) copy-start(f32[640]{0:T(1024)} %copy-done.45) | copy-start | bytes 7684
  317.0 45.6 %copy-start.31 = (bf16[128,1024]{1,0:T(8,128)(2,1)}, bf16[128,1024]{1,0:T(8,128)(2,1)S(1)}, u32[]{:S(2)}) copy-start(bf16[128,1024]{1,0:T(8,128)(2,1)S(1)} %get-tuple-element.493) | copy-start | bytes 786436
  365.9 4.9 copy-start.7
  393.9 44.0 %copy-start.67 = (f32[128]{0:T(128)S(1)}, f32[128]{0:T(128)}, u32[]{:S(2)}) copy-start(f32[128]{0:T(128)} %copy-done.66) | copy-start | bytes 1540
  393.9 44.0 %copy-start.69 = (f32[96]{0:T(128)S(1)}, f32[96]{0:T(128)}, u32[]{:S(2)}) copy-start(f32[96]{0:T(128)} %param.25) | copy-start | bytes 1156
  393.9 44.0 %copy-start.70 = (f32[96]{0:T(128)S(1)}, f32[96]{0:T(128)}, u32[]{:S(2)}) copy-start(f32[96]{0:T(128)} %param.28) | copy-start | bytes 1156
  393.9 44.0 %copy-start.71 = (f32[96]{0:T(128)S(1)}, f32[96]{0:T(128)}, u32[]{:S(2)}) copy-start(f32[96]{0:T(128)} %param.29) | copy-start | bytes 1156
  393.9 44.6 %copy-start.20 = (f32[128,640]{1,0:T(8,128)S(1)}, f32[128,640]{1,0:T(8,128)}, u32[]{:S(2)}) copy-start(f32[128,640]{1,0:T(8,128)} %copy-done.19) | copy-start | bytes 983044
  (44 other events, 71.3 us)
Sparse Core Ops, SparseCore 0:
  11.4 93.0 all-gather.3
  112.2 36.4 all-gather.7
  150.8 36.8 all-gather.5
  287.0 71.2 reduce-scatter.1
  394.0 356.7 all-reduce.4
where the time goes:
time: 772 us; the launch traced here: 761 us
  waiting for transfers between devices  434 us (56%)
  local copies, waits for them, and re-layouts  120 us (16%)
  blocking collectives  84.2 us (11%)
  other arithmetic  59.1 us (8%)
  matrix products  35.5 us (5%)
  between operations  16.5 us (2%)
  loops' own time  11.5 us (1%)
    unnamed x6, waiting for transfers between devices  311 us
    unnamed x2, blocking collectives  84.2 us
    all_gather x1, waiting for transfers between devices, shards(): lax.all_gather(matrices.astype(jnp.bfloat16), ('ctx', 'fsdp'), axis=0, ti...  47.5 us
    reduce_scatter x1, waiting for transfers between devices, shards(): lax.psum_scatter(slot_terms, 'ctx', scatter_dimension=0, tiled=True)  41.3 us
    all_gather x1, waiting for transfers between devices, shards(): lax.all_gather(key_blocks, 'ctx', axis=0, tiled=True)  34.1 us
    concatenate x1, other arithmetic, shards(): jnp.concatenate([grad_wqkv.reshape(-1), grad_wout.reshape(-1), grad_gateu...  23 us
    unnamed x148, local copies, waits for them, and re-layouts  16.5 us
  transfers between devices with their start and end apart: 5, of which 4 were waited for; matrix products, arithmetic and copies ran while one was open for 10% of the time, Pallas kernels for 0%

commit v1 on v0

--- a/solution.py
+++ b/solution.py
@@ -9,6 +9,7 @@
 FF = 2048
 BLK = 64
 STEP = 3
+LANES = 128
 
 
 NORM_EPS = 1e-06
@@ -151,9 +152,11 @@
     gain_first,
     gain_second,
 ):
-    gathered, gains_low = (
-        lax.all_gather(matrices.astype(jnp.bfloat16), ("ctx", "fsdp"), axis=0, tiled=True),
-        lax.all_gather(gain_offsets.astype(jnp.bfloat16), ("ctx", "fsdp"), axis=0, tiled=True),
+    gathered = lax.all_gather(
+        matrices.astype(jnp.bfloat16).reshape(-1, LANES), ("ctx", "fsdp"), axis=0, tiled=True
+    ).reshape(-1)
+    gains_low = lax.all_gather(
+        gain_offsets.astype(jnp.bfloat16), ("ctx", "fsdp"), axis=0, tiled=True
     )
     w_qkv, w_out, w_gateup, w_down = split_weights(gathered)
     gain_in, gain_query, gain_key, gain_attn, gain_ffn, gain_post = split_gains(
@@ -195,10 +198,9 @@
         .astype(jnp.bfloat16)
         .reshape(query_count, HD)
     )
-    key_blocks = (
-        rotate(key_normed, cosine_table, sine_table).astype(jnp.bfloat16).reshape(2, BLK, HD)
-    )
-    value_blocks = value_raw.astype(jnp.bfloat16).reshape(2, BLK, HD)
+    own_keyval = jnp.concatenate(
+        [rotate(key_normed, cosine_table, sine_table), value_raw], axis=1
+    ).astype(jnp.bfloat16)
     upper_queries = lax.dynamic_slice_in_dim(query_rows, upper_start, upper_span, 0)
     upper_order = lax.dynamic_slice_in_dim(query_order, upper_start, upper_span, 0)
 
@@ -238,15 +240,15 @@
         jnp.zeros((query_count,), jnp.float32),
         jnp.zeros((query_count, HD), jnp.float32),
     )
-    all_keys, all_values = (
-        lax.all_gather(key_blocks, "ctx", axis=0, tiled=True),
-        lax.all_gather(value_blocks, "ctx", axis=0, tiled=True),
+    all_keyval = lax.all_gather(
+        own_keyval.reshape(2, BLK, 2 * HD), "ctx", axis=0, tiled=True
     )
     inverse = jnp.sum(
         jnp.where(block_map[None, :] == block_ids[:, None], block_ids[None, :], 0), axis=1
     )
-    sorted_keys = all_keys[inverse].reshape(group_count, group_keys, HD)
-    sorted_values = all_values[inverse].reshape(group_count, group_keys, HD)
+    sorted_keyval = all_keyval[inverse].reshape(group_count, group_keys, 2 * HD)
+    sorted_keys = sorted_keyval[:, :, :HD]
+    sorted_values = sorted_keyval[:, :, HD:]
 
     def kept_forward(inner, scan_item):
         key_rows, value_rows, group_id = scan_item
@@ -346,10 +348,10 @@
         kept_backward, init_backward, (sorted_keys, sorted_values, group_index)
     )
     grad_query_all, seq_terms = backward_state
-    slot_terms = seq_terms.reshape(num_blocks, BLK, 2 * HD)[block_map]
+    slot_terms = seq_terms.astype(jnp.bfloat16).reshape(num_blocks, BLK, 2 * HD)[block_map]
     key_terms = lax.psum_scatter(slot_terms, "ctx", scatter_dimension=0, tiled=True).reshape(
         token_rows, 2 * HD
-    )
+    ).astype(jnp.float32)
     grad_key_rot = key_terms[:, :HD]
     grad_value = key_terms[:, HD:]
     grad_query_rot = grad_query_all.reshape(token_rows, HEADS, HD)
@@ -384,10 +386,18 @@
             grad_gain_post,
         ]
     )
-    matrix_grad, gain_grad = (
-        lax.psum_scatter(local_matrix, ("ctx", "fsdp"), scatter_dimension=0, tiled=True),
-        lax.psum_scatter(local_gain, ("ctx", "fsdp"), scatter_dimension=0, tiled=True),
-    )
+    device_count = gathered.shape[0] // matrices.shape[0]
+    matrix_grad = (
+        lax.psum_scatter(
+            local_matrix.astype(jnp.bfloat16).reshape(device_count, -1, LANES),
+            ("ctx", "fsdp"),
+            scatter_dimension=0,
+            tiled=True,
+        )
+        .reshape(-1)
+        .astype(jnp.float32)
+    )
+    gain_grad = lax.psum_scatter(local_gain, ("ctx", "fsdp"), scatter_dimension=0, tiled=True)
     new_matrices, new_first, new_second = adamw_update(
         matrices, first_moment, second_moment, matrix_grad
     )

time: 772 us -> 623 us (0.81)
  waiting for transfers between devices: 434 us -> 286 us
  other arithmetic: 59.1 us -> 72.7 us
  local copies, waits for them, and re-layouts: 120 us -> 109 us
    unnamed x6 -> x4, waiting for transfers between devices: 311 us -> 0.07 us
    reduce_scatter x0 -> x1, waiting for transfers between devices: none -> 197 us  [shards(): lax.psum_scatter(local_matrix.astype(jnp.bfloat16).reshape(device_count,...]
    all_gather x3 -> x2, waiting for transfers between devices: 81.6 us -> 52.5 us  [the longest x1 49.5 us: shards(): lax.all_gather(matrices.astype(jnp.bfloat16).reshape(-1, LANES), ('ctx',...]
    reshape x0 -> x3, local copies, waits for them, and re-layouts: none -> 15.3 us  [the longest x1 8.84 us: split_weights(): flat_values[second_end:third_end].reshape(D, 2 * FF)]
    concatenate x1, other arithmetic: 23 us -> 34.9 us  [shards(): jnp.concatenate([grad_wqkv.reshape(-1), grad_wout.reshape(-1), grad_gateu...]
    slice x2 -> x1, local copies, waits for them, and re-layouts: 14.6 us -> 5.79 us  [split_weights(): flat_values[second_end:third_end].reshape(D, 2 * FF)]
    unnamed x148 -> x156, local copies, waits for them, and re-layouts: 16.5 us -> 14.7 us
  transfers between devices with their start and end apart: 5 -> 4, of which waited for: 4 -> 4; matrix products, arithmetic and copies ran while one was open for 10% -> 10% of each run, Pallas kernels for 0% -> 0%
where the time goes in v1:
time: 623 us; the launch traced here: 613 us
  waiting for transfers between devices  286 us (46%)
  local copies, waits for them, and re-layouts  109 us (17%)
  blocking collectives  84.6 us (14%)
  other arithmetic  72.7 us (12%)
  matrix products  32.7 us (5%)
  between operations  16.5 us (3%)
  loops' own time  10.9 us (2%)
    reduce_scatter x1, waiting for transfers between devices, shards(): lax.psum_scatter(local_matrix.astype(jnp.bfloat16).reshape(device_count,...  197 us
    unnamed x2, blocking collectives  84.6 us
    all_gather x1, waiting for transfers between devices, shards(): lax.all_gather(matrices.astype(jnp.bfloat16).reshape(-1, LANES), ('ctx',...  49.5 us
    reduce_scatter x1, waiting for transfers between devices, shards(): lax.psum_scatter(slot_terms, 'ctx', scatter_dimension=0, tiled=True)  36.4 us
    concatenate x1, other arithmetic, shards(): jnp.concatenate([grad_wqkv.reshape(-1), grad_wout.reshape(-1), grad_gateu...  34.9 us
    unnamed x156, local copies, waits for them, and re-layouts  14.7 us
  transfers between devices with their start and end apart: 4, of which 4 were waited for; matrix products, arithmetic and copies ran while one was open for 10% of the time, Pallas kernels for 0%

profile of v1, /device:TPU:0, one launch (start us, length us, event | category | flops | bytes accessed | tf_op | source)
XLA Modules:
  0.0 613.0 jit_solution(7147127643405671223)
XLA Ops:
  7.2 1.9 convert_bitcast_fusion
  10.0 42.6 %all-reduce = bf16[3072]{0:T(1024)(128)(2,1)S(1)} all-reduce(bf16[3072]{0:T(1024)(128)(2,1)S(1)} %dynamic-update-slice), channel_id=1, replica_groups=mesh['ctx'=16,'fsdp'=2] {'ctx','fsdp'}, use_global_device_ids=true, to_apply=%add | all-reduce | flops 3072 | bytes 12288
  55.0 49.5 %all-gather.3.cloned.1.call-done = bf16[43520,128]{1,0:T(8,128)(2,1)} async-done(((bf16[1360,128]{1,0:T(8,128)(2,1)}), bf16[43520,128]{1,0:T(8,128)(2,1)}) %all-gather.3.cloned.1.call-update) | async-done | bytes 11141136 | tf_op jit(solution)/shard_map/all_gather | solution.py:155
  104.6 1.5 slice-done.2
  106.1 3.2 reshape.331
  109.4 2.1 fusion.48
  125.8 5.8 slice.146
  131.6 8.8 %reshape.338 = bf16[640,4096]{1,0:T(8,128)(2,1)} reshape(bf16[20480,128]{1,0:T(8,128)(2,1)} %slice.146) | data formatting | bytes 10485760 | tf_op jit(solution)/shard_map/reshape | solution.py:74
  140.5 2.9 slice.149
  143.3 5.5 reshape.339
  151.7 3.0 all-gather.5.cloned.1.call-done
  154.7 2.4 gather_fusion
  158.6 20.6 %while.31 = (s32[]{:T(128)}, f32[512]{0:T(512)S(1)}, f32[512]{0:T(512)S(1)}, f32[512,256]{1,0:T(8,128)S(1)}, s32[2]{0:T(128)S(1)}, /*index=5*/s32[]{:T(128)}, s3...) while((s32[]{:T(128)}, f32[512]{0:T(512)S(1)}, ...), condition=%wide.region_15.16_spmd.clone, body=%wide.region_7.15_spmd.clone.sunk | while | flops 542902272 | bytes 10814449 | solution.py:261
  163.1 5.7 conditional.6
  167.2 1.6 convolution_add_fusion
  174.1 4.3 conditional.6
  180.5 3.6 fusion.72
  190.6 2.4 multiply_reduce_fusion.4
  197.8 2.5 broadcast_in_dim.90.clone
  200.4 46.2 %while.32 = (s32[]{:T(128)}, f32[512,256]{1,0:T(8,128)}, f32[2048,512]{1,0:T(8,128)}, s32[2]{0:T(128)S(1)}, s32[]{:T(128)}, /*index=5*/s32[]{:T(128)}, bf16[2,10...) while((s32[]{:T(128)}, f32[512,256]{1,0:T(8,128)}, ...), condition=%wide.region_27.28_spmd.clone, body=%wide.region_23.27_spmd.clone.sunk | while | flops 1347027968 | bytes 45655392 | solution.py:347
  204.7 6.6 %conditional.7 = (f32[512,256]{1,0:T(8,128)}, f32[1024,512]{0,1:T(8,128)S(1)}) conditional(s32[]{:T(128)} %clamp.15, (s32[1024]{0:T(1024)S(1)}, s32[128]{0:T(128)S(1)}, bf16[1024,256]{1,0:T(8,128)(2,1)S(1)}, bf16[512,256]{1,0:T(8,128)(2,1)}, f32[512]{0:T(512)}, /*index=5*/bf16[1024,256]{1,0:T(8,128)(2,1)S(1)}, ...), branch_computations={%region_24.24_spmd, %region_25.25_spmd, %region_26.26_spmd} | conditional | flops 1346502656 | bytes 19415568 | solution.py:333
  207.4 2.3 convolution_add_fusion.2
  211.3 3.1 constant_dynamic-slice_fusion.4
  214.5 3.0 copy.64
  217.5 3.4 add.471
  220.8 1.9 copy.65
  228.8 4.7 conditional.7
  231.2 1.7 dynamic_update_slice.13
  233.5 3.1 constant_dynamic-slice_fusion.4
  236.7 3.0 copy.64
  239.6 3.4 add.471
  243.0 1.9 copy.65
  246.5 2.5 convert_element_type.111
  249.0 2.2 gather_fusion.1
  254.1 2.0 reshape.342
  256.1 2.0 reshape.341
  258.6 2.0 reshape.345
  260.6 1.8 convolution_convert_fusion.2
  262.4 3.3 reshape.347
  265.7 2.7 fusion.25
  268.4 3.9 copy.61
  276.1 36.4 %reduce-scatter.3.cloned.1.call-done = bf16[2,64,512]{2,1,0:T(8,128)(2,1)} async-done(((bf16[32,64,512]{2,1,0:T(8,128)(2,1)}), bf16[2,64,512]{2,1,0:T(8,128)(2,1)}) %reduce-scatter.3.cloned.1.call-update) | async-done | bytes 131088 | tf_op jit(solution)/shard_map/reduce_scatter | solution.py:352
  316.2 3.0 convolution_convert_fusion.1
  319.2 5.1 reshape.344
  324.4 34.9 %pad_maximum_fusion.2 = bf16[5570560]{0:T(1024)(128)(2,1)} fusion(bf16[1310720]{0:T(1024)(128)(2,1)S(1)} %copy-done.7, bf16[2621440]{0:T(1024)(128)(2,1)} %bitcast.138, bf16[655360]{0:T(1024)(128)(2,1)} %reshape.345, bf16[983040]{0:T(1024)(128)(2,1)} %reshape.344), kind=kLoop, calls=%fused_computation.50 | loop fusion | flops 44564480 | bytes 22282240 | tf_op jit(solution)/shard_map/concatenate | solution.py:371
  361.7 42.1 %all-reduce.1 = f32[3072]{0:T(1024)S(1)} all-reduce(f32[3072]{0:T(1024)S(1)} %constant_dynamic-update-slice_fusion.1), channel_id=4, replica_groups=mesh['ctx'=16,'fsdp'=2] {'ctx','fsdp'}, use_global_device_ids=true, to_apply=%region_40.41.clone | all-reduce | flops 3072 | bytes 24576
  405.3 197.4 %reduce-scatter.5.cloned.1.call-done = bf16[1,1360,128]{2,1,0:T(8,128)(2,1)} async-done(((bf16[32,1360,128]{2,1,0:T(8,128)(2,1)}), bf16[1,1360,128]{2,1,0:T(8,128)(2,1)}) %reduce-scatter.5.cloned.1.call-update) | async-done | bytes 348176 | tf_op jit(solution)/shard_map/reduce_scatter | solution.py:391
  602.7 3.3 multiply_subtract_fusion
  (355 shorter events, 74.8 us)
Async XLA Ops:
  7.2 97.4 %all-gather.3.cloned.1.call-start = ((), (), s32[]{:S(2)}) async-start(), calls=%async_computation.2 | async-start | bytes 11489280 | tf_op jit(solution)/shard_map/all_gather | solution.py:155
  9.1 145.6 %all-gather.5.cloned.1.call-start = ((), (), s32[]{:S(2)}) async-start(), calls=%async_computation.3 | async-start | bytes 2228224 | tf_op jit(solution)/shard_map/all_gather | solution.py:243
  53.7 55.6 %copy-start.66 = (f32[128]{0:T(128)}, f32[128]{0:T(128)S(1)}, u32[]{:S(2)}) copy-start(f32[128]{0:T(128)S(1)} %fusion.63) | copy-start | bytes 1540
  54.4 58.2 %copy-start.56 = (f32[256]{0:T(256)}, f32[256]{0:T(256)S(1)}, u32[]{:S(2)}) copy-start(f32[256]{0:T(256)S(1)} %get-tuple-element.517) | copy-start | bytes 3076
  54.4 94.8 %copy-start.54 = (f32[256]{0:T(256)}, f32[256]{0:T(256)S(1)}, u32[]{:S(2)}) copy-start(f32[256]{0:T(256)S(1)} %get-tuple-element.516) | copy-start | bytes 3076
  55.0 54.3 %copy-start.46 = (f32[640]{0:T(1024)}, f32[640]{0:T(1024)S(1)}, u32[]{:S(2)}) copy-start(f32[640]{0:T(1024)S(1)} %get-tuple-element.515) | copy-start | bytes 7684
  106.1 3.3 copy-start.12
  109.4 5.4 copy-start.78
  111.4 8.5 %copy-start.10 = (f32[128,1536]{1,0:T(8,128)}, f32[128,1536]{1,0:T(8,128)S(1)}, u32[]{:S(2)}) copy-start(f32[128,1536]{1,0:T(8,128)S(1)} %fusion.48) | copy-start | bytes 2359300
  111.6 7.7 %copy-start.64 = (f32[128]{0:T(128)}, f32[128]{0:T(128)S(1)}, u32[]{:S(2)}) copy-start(f32[128]{0:T(128)S(1)} %fusion.64) | copy-start | bytes 1540
  114.7 197.8 %reduce-scatter.3.cloned.1.call-start = ((), (), s32[]{:S(2)}) async-start(), calls=%async_computation.4 | async-start | bytes 2228224 | tf_op jit(solution)/shard_map/reduce_scatter | solution.py:352
  120.2 28.7 %copy-start.8 = (f32[128,4,256]{2,1,0:T(4,128)}, f32[128,4,256]{2,1,0:T(4,128)S(1)}, u32[]{:S(2)}) copy-start(f32[128,4,256]{2,1,0:T(4,128)S(1)} %reshape.334) | copy-start | bytes 1572868
  123.1 8.5 %copy-start.58 = (f32[128,4]{0,1:T(4,128)}, f32[128,4]{0,1:T(4,128)S(1)}, u32[]{:S(2)}) copy-start(f32[128,4]{0,1:T(4,128)S(1)} %copy.27) | copy-start | bytes 6148
  123.3 25.6 %copy-start.32 = (f32[128,4]{1,0:T(8,128)}, f32[128,4]{1,0:T(8,128)S(1)}, u32[]{:S(2)}) copy-start(f32[128,4]{1,0:T(8,128)S(1)} %copy.28) | copy-start | bytes 6148
  158.6 4.5 copy-start.51
  169.6 4.5 copy-start.51
  179.6 4.5 copy-start.22
  180.4 12.6 %copy-start.4 = (f32[128,640]{1,0:T(8,128)}, f32[128,640]{1,0:T(8,128)S(1)}, u32[]{:S(2)}) copy-start(f32[128,640]{1,0:T(8,128)S(1)} %get-tuple-element.480) | copy-start | bytes 983044
  180.5 12.6 %copy-start.62 = (f32[128]{0:T(128)}, f32[128]{0:T(128)S(1)}, u32[]{:S(2)}) copy-start(f32[128]{0:T(128)S(1)} %fusion.66) | copy-start | bytes 1540
  194.7 5.6 copy-start.28
  200.4 4.4 copy-start
  200.4 4.4 copy-start.48
  200.4 4.4 copy-start.69
  224.4 4.4 copy-start
  224.4 4.4 copy-start.48
  224.4 4.4 copy-start.69
  251.2 351.6 %reduce-scatter.5.cloned.1.call-start = ((), (), s32[]{:S(2)}) async-start(), calls=%async_computation.5 | async-start | bytes 11489280 | tf_op jit(solution)/shard_map/reduce_scatter | solution.py:391
  253.1 5.0 copy-start.23
  253.1 5.0 copy-start.29
  262.4 3.3 copy-start.5
  262.4 3.3 copy-start.44
  262.4 3.3 copy-start.63
  268.4 4.0 copy-start.18
  268.4 4.0 copy-start.40
  274.4 39.0 %copy-start.39 = (f32[128,128]{1,0:T(8,128)S(1)}, f32[128,128]{1,0:T(8,128)}, u32[]{:S(2)}) copy-start(f32[128,128]{1,0:T(8,128)} %copy-done.38) | copy-start | bytes 196612
  274.5 39.7 %copy-start.35 = (f32[128,128]{1,0:T(8,128)S(1)}, f32[128,128]{1,0:T(8,128)}, u32[]{:S(2)}) copy-start(f32[128,128]{1,0:T(8,128)} %copy-done.34) | copy-start | bytes 196612
  274.5 39.7 %copy-start.57 = (f32[256]{0:T(256)S(1)}, f32[256]{0:T(256)}, u32[]{:S(2)}) copy-start(f32[256]{0:T(256)} %copy-done.56) | copy-start | bytes 3076
  274.5 39.7 %copy-start.65 = (f32[128]{0:T(128)S(1)}, f32[128]{0:T(128)}, u32[]{:S(2)}) copy-start(f32[128]{0:T(128)} %copy-done.64) | copy-start | bytes 1540
  275.0 40.2 %copy-start.74 = (f32[128]{0:T(128)S(1)}, f32[128]{0:T(128)}, u32[]{:S(2)}) copy-start(f32[128]{0:T(128)} %copy-done.73) | copy-start | bytes 1540
  275.0 41.2 %copy-start.14 = (f32[1,128,640]{2,1,0:T(8,128)S(1)}, f32[1,128,640]{2,1,0:T(8,128)}, u32[]{:S(2)}) copy-start(f32[1,128,640]{2,1,0:T(8,128)} %param.20) | copy-start | bytes 983044
  275.0 41.2 %copy-start.47 = (f32[640]{0:T(1024)S(1)}, f32[640]{0:T(1024)}, u32[]{:S(2)}) copy-start(f32[640]{0:T(1024)} %copy-done.46) | copy-start | bytes 7684
  275.0 41.2 %copy-start.67 = (f32[128]{0:T(128)S(1)}, f32[128]{0:T(128)}, u32[]{:S(2)}) copy-start(f32[128]{0:T(128)} %copy-done.66) | copy-start | bytes 1540
  319.2 5.1 copy-start.7
  359.3 44.5 %copy-start.72 = (f32[128]{0:T(128)S(1)}, f32[128]{0:T(128)}, u32[]{:S(2)}) copy-start(f32[128]{0:T(128)} %copy-done.71) | copy-start | bytes 1540
  359.3 44.5 %copy-start.75 = (f32[96]{0:T(128)S(1)}, f32[96]{0:T(128)}, u32[]{:S(2)}) copy-start(f32[96]{0:T(128)} %param.25) | copy-start | bytes 1156
  359.4 44.5 %copy-start.76 = (f32[96]{0:T(128)S(1)}, f32[96]{0:T(128)}, u32[]{:S(2)}) copy-start(f32[96]{0:T(128)} %param.28) | copy-start | bytes 1156
  359.4 44.5 %copy-start.77 = (f32[96]{0:T(128)S(1)}, f32[96]{0:T(128)}, u32[]{:S(2)}) copy-start(f32[96]{0:T(128)} %param.29) | copy-start | bytes 1156
  359.4 45.1 %copy-start.21 = (f32[128,640]{1,0:T(8,128)S(1)}, f32[128,640]{1,0:T(8,128)}, u32[]{:S(2)}) copy-start(f32[128,640]{1,0:T(8,128)} %copy-done.20) | copy-start | bytes 983044
  (51 other events, 83.5 us)
Sparse Core Ops, SparseCore 0:
  11.4 93.0 all-gather.2
  114.8 39.8 all-gather.4
  251.3 61.1 reduce-scatter.2
  359.4 243.2 reduce-scatter.4

commit v2 on v1

--- a/solution.py
+++ b/solution.py
@@ -1,6 +1,10 @@
+import functools
+
 import jax
 import jax.numpy as jnp
 from jax import lax
+from jax.experimental import pallas as pl
+from jax.experimental.pallas import tpu as pltpu
 from jax.sharding import PartitionSpec as P
 
 D = 640
@@ -9,7 +13,6 @@
 FF = 2048
 BLK = 64
 STEP = 3
-LANES = 128
 
 
 NORM_EPS = 1e-06
@@ -19,6 +22,295 @@
 BETA_TWO = 0.95
 ADAM_EPS = 1e-08
 DECAY_RATE = 0.1
+
+LANES = 128
+ROW_TILE = 16
+
+
+def bit_of(index, bit):
+    return lax.rem(index // (1 << bit), 2)
+
+
+def flipped(index, bit):
+    return index + (1 - 2 * bit_of(index, bit)) * (1 << bit)
+
+
+def compress(index, bits):
+    slot = 0
+    for rank, bit in enumerate(bits):
+        slot = slot + bit_of(index, bit) * (1 << rank)
+    return slot
+
+
+class Group:
+    def __init__(self, ctx_size, fsdp_size, whole):
+        self.fsdp_size = fsdp_size
+        self.whole = whole
+        self.size = ctx_size * fsdp_size if whole else ctx_size
+        self.bits = self.size.bit_length() - 1
+
+    def position(self):
+        if self.whole:
+            return lax.axis_index("ctx") * self.fsdp_size + lax.axis_index("fsdp")
+        return lax.axis_index("ctx")
+
+    def place(self, index):
+        if self.whole:
+            return (index // self.fsdp_size, lax.rem(index, self.fsdp_size))
+        return (index, lax.axis_index("fsdp"))
+
+    def orders(self):
+        if self.whole:
+            upper = list(range(3, self.bits))
+            return ([1, 2, 0] + upper, [1, 0] + upper + [2])
+        upper = list(range(2, self.bits))
+        return ([0, 1] + upper, [0] + upper + [1])
+
+
+def row_parts(rows, share=9):
+    middle = max(1, rows * share // 16 // ROW_TILE) * ROW_TILE
+    return ((0, middle), (middle, rows - middle))
+
+
+def enter(group, me):
+    barrier = pltpu.get_barrier_semaphore()
+    for bit in range(group.bits):
+        pl.semaphore_signal(
+            barrier,
+            inc=1,
+            device_id=group.place(flipped(me, bit)),
+            device_id_type=pl.DeviceIdType.MESH,
+        )
+    pl.semaphore_wait(barrier, group.bits)
+
+
+def gather_kernel(group, parts, array_count, *refs):
+    own_refs = refs[:array_count]
+    out_refs = refs[array_count : 2 * array_count]
+    local_sem, send_sem, recv_sem = refs[2 * array_count :]
+    me = group.position()
+    enter(group, me)
+    orders = [part[3][::-1] for part in parts]
+    locals_ = []
+    for number in range(array_count):
+        copy = pltpu.make_async_copy(
+            own_refs[number], out_refs[number].at[me], local_sem.at[number]
+        )
+        copy.start()
+        locals_.append(copy)
+
+    def transfer(part, block, step, own=False):
+        number, first, count, _ = parts[part]
+        rows = pl.ds(first, count)
+        target = out_refs[number].at[block, rows]
+        return pltpu.make_async_remote_copy(
+            src_ref=own_refs[number].at[rows] if own else target,
+            dst_ref=target,
+            send_sem=send_sem.at[part, (1 << step) + compress(block, orders[part][:step])],
+            recv_sem=recv_sem.at[part, block],
+            device_id=group.place(flipped(me, orders[part][step])),
+            device_id_type=pl.DeviceIdType.MESH,
+        )
+
+    def block_at(part, step, count):
+        block = flipped(me, orders[part][step])
+        for rank in range(step):
+            bit = orders[part][rank]
+            block = block + bit_of(count, rank) * (1 - 2 * bit_of(me, bit)) * (1 << bit)
+        return block
+
+    for step in range(group.bits):
+        for part in range(len(parts)):
+            transfer(part, me, step, True).start()
+    for step in range(group.bits):
+
+        def arrived(count, carried, step=step):
+            for part in range(len(parts)):
+                block = block_at(part, step, count)
+                transfer(part, block, step).wait_recv()
+                for later in range(step + 1, group.bits):
+                    transfer(part, block, later).start()
+            return carried
+
+        lax.fori_loop(0, 1 << step, arrived, 0)
+    for copy in locals_:
+        copy.wait()
+    for step in range(group.bits):
+        for part in range(len(parts)):
+            transfer(part, me, step, True).wait_send()
+    for step in range(group.bits - 1):
+
+        def sent(count, carried, step=step):
+            for part in range(len(parts)):
+                block = block_at(part, step, count)
+                for later in range(step + 1, group.bits):
+                    transfer(part, block, later).wait_send()
+            return carried
+
+        lax.fori_loop(0, 1 << step, sent, 0)
+
+
+def gather_all(group, parts, owns, collective_id):
+    any_spec = pl.BlockSpec(memory_space=pl.ANY)
+    return pl.pallas_call(
+        functools.partial(gather_kernel, group, parts, len(owns)),
+        out_shape=[jax.ShapeDtypeStruct((group.size,) + own.shape, own.dtype) for own in owns],
+        in_specs=[any_spec] * len(owns),
+        out_specs=[any_spec] * len(owns),
+        scratch_shapes=[
+            pltpu.SemaphoreType.DMA((len(owns),)),
+            pltpu.SemaphoreType.DMA((len(parts), group.size)),
+            pltpu.SemaphoreType.DMA((len(parts), group.size)),
+        ],
+        compiler_params=pltpu.CompilerParams(
+            collective_id=collective_id, has_side_effects=True
+        ),
+    )(*owns)
+
+
+def reduce_kernel(group, parts, piece_rows, array_count, *refs):
+    piece_count = sum(len(rows) for rows in piece_rows)
+    piece_refs = refs[:piece_count]
+    out_refs = refs[piece_count : piece_count + array_count]
+    refs = refs[piece_count + array_count :]
+    term_refs, refs = refs[:array_count], refs[array_count:]
+    held = [
+        refs[part * group.bits : (part + 1) * group.bits] for part in range(len(parts))
+    ]
+    local_sem, send_sem, recv_sem = refs[len(parts) * group.bits :]
+    me = group.position()
+    copies = []
+    for number in range(array_count):
+        first = 0
+        for rows in piece_rows[number]:
+            copy = pltpu.make_async_copy(
+                piece_refs[len(copies)],
+                term_refs[number].at[pl.ds(first, rows)],
+                local_sem.at[len(copies)],
+            )
+            copy.start()
+            copies.append(copy)
+            first += rows
+    enter(group, me)
+    for copy in copies:
+        copy.wait()
+    orders = [part[3] for part in parts]
+
+    def source_of(part, step, block):
+        number, first, count, _ = parts[part]
+        if step == 0:
+            each = term_refs[number].shape[0] // group.size
+            start = pl.multiple_of(block * each + first, first_tile(first, each))
+            return term_refs[number].at[pl.ds(start, count)]
+        return held[part][step - 1].at[compress(block, orders[part][step:])]
+
+    def transfer(part, step, block):
+        slot = compress(block, orders[part][step + 1 :])
+        return pltpu.make_async_remote_copy(
+            src_ref=source_of(part, step, block),
+            dst_ref=held[part][step].at[slot],
+            send_sem=send_sem.at[part, block_count(step) + slot],
+            recv_sem=recv_sem.at[part, block_count(step) + slot],
+            device_id=group.place(flipped(me, orders[part][step])),
+            device_id_type=pl.DeviceIdType.MESH,
+        )
+
+    def block_at(part, step, count, away):
+        order = orders[part]
+        block = flipped(me, order[step]) if away else me
+        left = order[step + 1 :]
+        for rank, bit in enumerate(left):
+            chosen = bit_of(count, len(left) - 1 - rank)
+            block = block + chosen * (1 - 2 * bit_of(me, bit)) * (1 << bit)
+        return block
+
+    def block_count(step):
+        return 1 << (group.bits - 1 - step)
+
+    def first_sends(index, carried):
+        for part in range(len(parts)):
+            transfer(part, 0, block_at(part, 0, block_count(0) - 1 - index, True)).start()
+        return carried
+
+    lax.fori_loop(0, block_count(0), first_sends, 0)
+    for step in range(group.bits):
+        total = block_count(step)
+        last = step == group.bits - 1
+
+        def arrived(index, carried, step=step, total=total, last=last, onward=True):
+            for part in range(len(parts)):
+                number, first, count, _ = parts[part]
+                block = block_at(part, step, total - 1 - index, False)
+                transfer(part, step, block).wait_recv()
+                slot = compress(block, orders[part][step + 1 :])
+                mine = source_of(part, step, block)[...].astype(jnp.float32)
+                summed = held[part][step][slot].astype(jnp.float32) + mine
+                if last:
+                    out_refs[number][pl.ds(first, count), :] = summed
+                else:
+                    held[part][step][slot] = summed.astype(held[part][step].dtype)
+                    if onward:
+                        transfer(part, step + 1, block).start()
+            return carried
+
+        if last:
+            arrived(0, 0)
+        else:
+            lax.fori_loop(0, total // 2, arrived, 0)
+            lax.fori_loop(total // 2, total, functools.partial(arrived, onward=False), 0)
+    for step in range(group.bits):
+
+        def sent(count, carried, step=step):
+            for part in range(len(parts)):
+                transfer(part, step, block_at(part, step, count, True)).wait_send()
+            return carried
+
+        lax.fori_loop(0, block_count(step), sent, 0)
+
+
+def first_tile(first, each):
+    tile = ROW_TILE
+    while first % tile or each % tile:
+        tile //= 2
+    return tile
+
+
+def reduce_all(group, parts, pieces, collective_id):
+    flat = [piece for array in pieces for piece in array]
+    rows = [sum(piece.shape[0] for piece in array) for array in pieces]
+    widths = [array[0].shape[1] for array in pieces]
+    types = [array[0].dtype for array in pieces]
+    return pl.pallas_call(
+        functools.partial(
+            reduce_kernel,
+            group,
+            parts,
+            [[piece.shape[0] for piece in array] for array in pieces],
+            len(pieces),
+        ),
+        out_shape=[
+            jax.ShapeDtypeStruct((total // group.size, width), jnp.float32)
+            for total, width in zip(rows, widths)
+        ],
+        in_specs=[pl.BlockSpec(memory_space=pl.ANY)] * len(flat),
+        out_specs=[pl.BlockSpec(memory_space=pltpu.VMEM)] * len(pieces),
+        scratch_shapes=[
+            pltpu.VMEM((total, width), kind) for total, width, kind in zip(rows, widths, types)
+        ]
+        + [
+            pltpu.VMEM((1 << (group.bits - 1 - step), count, widths[number]), types[number])
+            for number, _, count, _ in parts
+            for step in range(group.bits)
+        ]
+        + [
+            pltpu.SemaphoreType.DMA((len(flat),)),
+            pltpu.SemaphoreType.DMA((len(parts), group.size)),
+            pltpu.SemaphoreType.DMA((len(parts), group.size)),
+        ],
+        compiler_params=pltpu.CompilerParams(
+            collective_id=collective_id, has_side_effects=True, vmem_limit_bytes=56 << 20
+        ),
+    )(*flat)
 
 
 def rms_apply(values, offset):
@@ -152,12 +444,32 @@
     gain_first,
     gain_second,
 ):
-    gathered = lax.all_gather(
-        matrices.astype(jnp.bfloat16).reshape(-1, LANES), ("ctx", "fsdp"), axis=0, tiled=True
-    ).reshape(-1)
-    gains_low = lax.all_gather(
-        gain_offsets.astype(jnp.bfloat16), ("ctx", "fsdp"), axis=0, tiled=True
-    )
+    fsdp_size = lax.axis_size("fsdp")
+    every = Group(lax.axis_size("ctx"), fsdp_size, True)
+    sequence = Group(lax.axis_size("ctx"), fsdp_size, False)
+    shard_rows = matrices.shape[0] // LANES
+    padded_rows = -(-shard_rows // ROW_TILE) * ROW_TILE
+    extra_rows = padded_rows - shard_rows
+    (early, late), (order_a, order_b) = row_parts(padded_rows), every.orders()
+    shard_parts = ((0,) + early + (order_a,), (0,) + late + (order_b,))
+    gain_count = gain_offsets.shape[0]
+    own_gains = jnp.pad(
+        gain_offsets.astype(jnp.bfloat16).reshape(1, gain_count),
+        ((0, ROW_TILE - 1), (0, LANES - gain_count)),
+    )
+    gathered, gain_rows = gather_all(
+        every,
+        shard_parts + ((1, 0, ROW_TILE, order_a),),
+        [
+            jnp.pad(
+                matrices.astype(jnp.bfloat16).reshape(shard_rows, LANES), ((0, extra_rows), (0, 0))
+            ),
+            own_gains,
+        ],
+        0,
+    )
+    gathered = gathered[:, :shard_rows].reshape(-1)
+    gains_low = gain_rows[:, 0, :gain_count].reshape(-1)
     w_qkv, w_out, w_gateup, w_down = split_weights(gathered)
     gain_in, gain_query, gain_key, gain_attn, gain_ffn, gain_post = split_gains(
         gains_low.astype(jnp.float32)
@@ -240,9 +552,10 @@
         jnp.zeros((query_count,), jnp.float32),
         jnp.zeros((query_count, HD), jnp.float32),
     )
-    all_keyval = lax.all_gather(
-        own_keyval.reshape(2, BLK, 2 * HD), "ctx", axis=0, tiled=True
-    )
+    (early_kv, late_kv), (order_c, order_d) = row_parts(token_rows, 8), sequence.orders()
+    keyval_parts = ((0,) + early_kv + (order_c,), (0,) + late_kv + (order_d,))
+    (all_keyval,) = gather_all(sequence, keyval_parts, [own_keyval], 2)
+    all_keyval = all_keyval.reshape(num_blocks, BLK, 2 * HD)
     inverse = jnp.sum(
         jnp.where(block_map[None, :] == block_ids[:, None], block_ids[None, :], 0), axis=1
     )
@@ -349,9 +662,9 @@
     )
     grad_query_all, seq_terms = backward_state
     slot_terms = seq_terms.astype(jnp.bfloat16).reshape(num_blocks, BLK, 2 * HD)[block_map]
-    key_terms = lax.psum_scatter(slot_terms, "ctx", scatter_dimension=0, tiled=True).reshape(
-        token_rows, 2 * HD
-    ).astype(jnp.float32)
+    (key_terms,) = reduce_all(
+        sequence, keyval_parts, [[slot_terms.reshape(num_blocks * BLK, 2 * HD)]], 3
+    )
     grad_key_rot = key_terms[:, :HD]
     grad_value = key_terms[:, HD:]
     grad_query_rot = grad_query_all.reshape(token_rows, HEADS, HD)
@@ -368,14 +681,6 @@
     grad_normed_in = jnp.dot(grad_projected, w_qkv.T, preferred_element_type=jnp.float32)
     grad_in_part, grad_gain_in = norm_back(residual_in, gain_in, grad_normed_in)
     grad_input = grad_after + grad_in_part
-    local_matrix = jnp.concatenate(
-        [
-            grad_wqkv.reshape(-1),
-            grad_wout.reshape(-1),
-            grad_gateup.reshape(-1),
-            grad_down.reshape(-1),
-        ]
-    )
     local_gain = jnp.concatenate(
         [
             grad_gain_in,
@@ -386,18 +691,23 @@
             grad_gain_post,
         ]
     )
-    device_count = gathered.shape[0] // matrices.shape[0]
-    matrix_grad = (
-        lax.psum_scatter(
-            local_matrix.astype(jnp.bfloat16).reshape(device_count, -1, LANES),
-            ("ctx", "fsdp"),
-            scatter_dimension=0,
-            tiled=True,
-        )
-        .reshape(-1)
-        .astype(jnp.float32)
-    )
-    gain_grad = lax.psum_scatter(local_gain, ("ctx", "fsdp"), scatter_dimension=0, tiled=True)
+    gain_terms = jnp.pad(
+        local_gain.reshape(every.size, 1, gain_count), ((0, 0), (0, 7), (0, LANES - gain_count))
+    ).reshape(every.size * 8, LANES)
+    matrix_terms = [
+        term.astype(jnp.bfloat16).reshape(-1, LANES)
+        for term in (grad_wqkv, grad_wout, grad_gateup, grad_down)
+    ]
+    if extra_rows:
+        whole_terms = jnp.concatenate(matrix_terms).reshape(every.size, shard_rows, LANES)
+        matrix_terms = [
+            jnp.pad(whole_terms, ((0, 0), (0, extra_rows), (0, 0))).reshape(-1, LANES)
+        ]
+    matrix_rows, gain_sums = reduce_all(
+        every, shard_parts + ((1, 0, 8, order_a),), [matrix_terms, [gain_terms]], 1
+    )
+    matrix_grad = matrix_rows[:shard_rows].reshape(-1)
+    gain_grad = gain_sums[0, :gain_count]
     new_matrices, new_first, new_second = adamw_update(
         matrices, first_moment, second_moment, matrix_grad
     )

time: 623 us -> 390 us (0.63)
  waiting for transfers between devices: 286 us -> 0 us
  Pallas kernels: 0 us -> 169 us
  blocking collectives: 84.6 us -> 0 us
  other arithmetic: 72.7 us -> 35.6 us
  between operations: 16.5 us -> 3.41 us
  local copies, waits for them, and re-layouts: 109 us -> 119 us
  loops' own time: 10.9 us -> 20 us
    reduce_scatter x2 -> x0, waiting for transfers between devices: 234 us -> none  [the longest x1 197 us: shards(): lax.psum_scatter(local_matrix.astype(jnp.bfloat16).reshape(device_count,...]
    pallas_call x0 -> x4, Pallas kernels: none -> 169 us  [the longest x2 92 us: reduce_all(): pl.pallas_call(functools.partial(reduce_kernel, group, parts, [[piece.sha...]
    unnamed x2 -> x0, blocking collectives: 84.6 us -> none
    all_gather x2 -> x0, waiting for transfers between devices: 52.5 us -> none  [the longest x1 49.5 us: shards(): lax.all_gather(matrices.astype(jnp.bfloat16).reshape(-1, LANES), ('ctx',...]
    concatenate x1 -> x0, other arithmetic: 34.9 us -> none  [shards(): jnp.concatenate([grad_wqkv.reshape(-1), grad_wout.reshape(-1), grad_gateu...]
    slice x2 -> x1, local copies, waits for them, and re-layouts: 0.76 us -> 19.3 us  [split_weights(): flat_values[first_end:second_end].reshape(HEADS * HD, D)]
    slice x1, local copies, waits for them, and re-layouts: 5.79 us -> 17.5 us  [split_weights(): flat_values[second_end:third_end].reshape(D, 2 * FF)]
    unnamed x156 -> x144, local copies, waits for them, and re-layouts: 14.7 us -> 4.04 us
  transfers between devices with their start and end apart: 4 -> 0, of which waited for: 4 -> 0; matrix products, arithmetic and copies ran while one was open for 10% -> 0% of each run, Pallas kernels for 0% -> 0%
where the time goes in v2:
time: 390 us; the launch traced here: 383 us
  Pallas kernels  169 us (43%)
  local copies, waits for them, and re-layouts  119 us (31%)
  matrix products  36.6 us (9%)
  other arithmetic  35.6 us (9%)
  loops' own time  20 us (5%)
    pallas_call x2, Pallas kernels, reduce_all(): pl.pallas_call(functools.partial(reduce_kernel, group, parts, [[piece.sha...  92 us
    pallas_call x2, Pallas kernels, gather_all(): pl.pallas_call(functools.partial(gather_kernel, group, parts, len(owns)),...  76.9 us
    slice x1, local copies, waits for them, and re-layouts, split_weights(): flat_values[first_end:second_end].reshape(HEADS * HD, D)  19.3 us
    slice x1, local copies, waits for them, and re-layouts, split_weights(): flat_values[second_end:third_end].reshape(D, 2 * FF)  17.5 us
    reshape x4, local copies, waits for them, and re-layouts, shards(): term.astype(jnp.bfloat16).reshape(-1, LANES)  17.2 us
    another operation x1, loops' own time, shards(): lax.scan(kept_backward, init_backward, (sorted_keys, sorted_values, group...  14.5 us
    dynamic_slice x4, local copies, waits for them, and re-layouts, add_rows(): lax.dynamic_slice_in_dim(term_rows, first_row, tile_rows.shape[0], 0)  12.2 us
    dynamic_update_slice x5, local copies, waits for them, and re-layouts, add_rows(): lax.dynamic_update_slice_in_dim(term_rows, current + tile_rows, first_row...  8.73 us

profile of v2, /device:TPU:0, one launch (start us, length us, event | category | flops | bytes accessed | tf_op | source)
XLA Modules:
  0.0 383.4 jit_solution(4471974347741094144)
XLA Ops:
  0.6 1.9 convert_bitcast_fusion.refs_0_
  3.8 56.3 %shard_map.177 = (bf16[32,1360,128]{2,1,0:T(8,128)(2,1)}, bf16[32,16,128]{2,1,0:T(8,128)(2,1)}) custom-call(bf16[1360,128]{1,0:T(8,128)(2,1)} %convert_bitcast_fusion.refs_0_, bf16[16,128]{1,0:T(8,128)(2,1)} %pad.8.refs_1_), custom_call_target="tpu_custom_call" | custom-call | tf_op jit(solution)/shard_map/pallas_call | solution.py:155
  60.1 17.5 %slice.122 = bf16[1360,4096]{1,0:T(8,128)(2,1)} reshape(bf16[32,1360,128]{2,1,0:T(8,128)(2,1)} %get-tuple-element.307) | data formatting | bytes 22282240 | tf_op jit(solution)/shard_map/slice | solution.py:366
  79.4 2.9 slice.140
  82.4 3.8 reshape.329
  89.4 20.6 %shard_map.178 = bf16[16,128,512]{2,1,0:T(8,128)(2,1)} custom-call(bf16[128,512]{1,0:T(8,128)(2,1)} %pad_maximum_fusion.11.refs_0_), custom_call_target="tpu_custom_call" | custom-call | tf_op jit(solution)/shard_map/pallas_call | solution.py:155
  110.2 2.3 gather_fusion
  112.5 1.5 fusion.86
  116.7 1.8 fusion.47
  123.0 21.9 %while.31 = (s32[]{:T(128)}, f32[512]{0:T(512)S(1)}, f32[512]{0:T(512)S(1)}, f32[512,256]{1,0:T(8,128)S(1)}, s32[2]{0:T(128)S(1)}, /*index=5*/s32[]{:T(128)}, s3...) while((s32[]{:T(128)}, f32[512]{0:T(512)S(1)}, ...), condition=%wide.region_15.16_spmd.clone, body=%wide.region_7.15_spmd.clone.sunk | while | flops 542902272 | bytes 10810325 | solution.py:574
  127.5 6.4 %conditional.6 = (f32[512]{0:T(512)}, f32[512]{0:T(512)S(1)}, f32[512,256]{1,0:T(8,128)S(1)}) conditional(s32[]{:T(128)} %clamp.14, (s32[1024]{0:T(1024)S(1)}, s32[128]{0:T(128)}, bf16[1024,256]{1,0:T(8,128)(2,1)S(1)}, bf16[512,256]{1,0:T(8,128)(2,1)}, f32[512]{0:T(512)S(1)}, /*index=5*/f32[512]{0:T(512)S(1)}, ...), branch_computations={%region_8.10_spmd, %region_11.13_spmd, %region_14.14_spmd} | conditional | flops 542901248 | bytes 8704536 | solution.py:544
  132.2 1.6 convolution_add_fusion
  139.0 5.2 %conditional.6 = (f32[512]{0:T(512)}, f32[512]{0:T(512)S(1)}, f32[512,256]{1,0:T(8,128)S(1)}) conditional(s32[]{:T(128)} %clamp.14, (s32[1024]{0:T(1024)S(1)}, s32[128]{0:T(128)}, bf16[1024,256]{1,0:T(8,128)(2,1)S(1)}, bf16[512,256]{1,0:T(8,128)(2,1)}, f32[512]{0:T(512)S(1)}, /*index=5*/f32[512]{0:T(512)S(1)}, ...), branch_computations={%region_8.10_spmd, %region_11.13_spmd, %region_14.14_spmd} | conditional | flops 542901248 | bytes 8704536 | solution.py:544
  140.0 1.5 fusion.81
  142.3 1.9 dynamic_update_slice.12
  145.2 19.3 %slice.118 = bf16[8704,640]{1,0:T(8,128)(2,1)} reshape(bf16[32,1360,128]{2,1,0:T(8,128)(2,1)} %get-tuple-element.307) | data formatting | bytes 22282240 | tf_op jit(solution)/shard_map/slice | solution.py:365
  164.6 1.8 multiply_reduce_fusion.12
  166.6 3.6 fusion.27
  170.6 2.6 multiply_reduce_fusion.10
  174.9 3.2 fusion.42
  178.1 5.4 %multiply_reduce_fusion.4 = (f32[640]{0:T(1024)}, f32[128]{0:T(128)S(1)}, f32[128,640]{1,0:T(8,128)S(1)}) fusion(f32[128,640]{1,0:T(8,128)S(1)} %get-tuple-element.488, f32[128]{0:T(128)S(1)} %fusion.74, f32[640]{0:T(1024)S(1)} %get-tuple-element.521, bf16[1360,4096]{1,0:T(8,128)(2,1)} %slice.122, bf16[128,2048]{1,0:T(8,128)(2,1)S(1)} %get-tuple-element.498, ...), kind=kOutput, calls=%fused_computation.118 | convolution fusion | flops 673676544 | bytes 6952960 | tf_op jit(solution)/shard_map/dot_general | solution.py:598
  185.7 1.9 convolution_convert_fusion.4
  189.4 2.5 broadcast_in_dim.90.clone
  191.9 55.8 %while.32 = (s32[]{:T(128)}, f32[512,256]{1,0:T(8,128)S(1)}, f32[2048,512]{1,0:T(8,128)}, s32[2]{0:T(128)}, s32[]{:T(128)}, /*index=5*/s32[]{:T(128)}, bf16[2,10...) while((s32[]{:T(128)}, f32[512,256]{1,0:T(8,128)S(1)}, ...), condition=%wide.region_27.28_spmd.clone, body=%wide.region_23.27_spmd.clone.sunk | while | flops 1347027968 | bytes 45647024 | solution.py:660
  197.1 5.4 %conditional.7 = (f32[512,256]{1,0:T(8,128)S(1)}, f32[1024,512]{0,1:T(8,128)S(1)}) conditional(s32[]{:T(128)} %clamp.15, (s32[1024]{0:T(1024)S(1)}, s32[128]{0:T(128)}, bf16[1024,256]{1,0:T(8,128)(2,1)S(1)}, bf16[512,256]{1,0:T(8,128)(2,1)}, f32[512]{0:T(512)}, /*index=5*/bf16[1024,256]{1,0:T(8,128)(2,1)S(1)}, ...), branch_computations={%region_24.24_spmd, %region_25.25_spmd, %region_26.26_spmd} | conditional | flops 1346502656 | bytes 19415568 | solution.py:646
  197.9 1.5 exponential_select_fusion
  202.5 3.1 constant_dynamic-slice_fusion.4
  205.6 3.0 copy.63
  208.6 3.4 add.463
  212.0 1.9 copy.64
  214.0 1.5 constant_dynamic-update-slice_fusion.8
  220.7 4.8 %conditional.7 = (f32[512,256]{1,0:T(8,128)S(1)}, f32[1024,512]{0,1:T(8,128)S(1)}) conditional(s32[]{:T(128)} %clamp.15, (s32[1024]{0:T(1024)S(1)}, s32[128]{0:T(128)}, bf16[1024,256]{1,0:T(8,128)(2,1)S(1)}, bf16[512,256]{1,0:T(8,128)(2,1)}, f32[512]{0:T(512)}, /*index=5*/bf16[1024,256]{1,0:T(8,128)(2,1)S(1)}, ...), branch_computations={%region_24.24_spmd, %region_25.25_spmd, %region_26.26_spmd} | conditional | flops 1346502656 | bytes 19415568 | solution.py:646
  222.8 1.9 dynamic_update_slice.13
  225.5 3.1 constant_dynamic-slice_fusion.4
  228.7 3.0 copy.63
  231.7 3.4 add.463
  235.0 1.9 copy.64
  237.0 1.5 constant_dynamic-update-slice_fusion.8
  247.7 2.5 convert_element_type.115
  250.2 2.0 gather_fusion.1
  252.3 21.4 %shard_map.179 = f32[128,512]{1,0:T(8,128)} custom-call(bf16[2048,512]{1,0:T(8,128)(2,1)} %bitcast.134), custom_call_target="tpu_custom_call" | custom-call | tf_op jit(solution)/shard_map/pallas_call | solution.py:283
  283.9 3.2 reshape.341.refs_0_
  287.8 1.8 reshape.342.refs_1_
  289.6 4.0 %convolution_convert_fusion = bf16[640,4096]{1,0:T(8,128)(2,1)} fusion(bf16[128,2048]{1,0:T(8,128)(2,1)S(1)} %copy-done.40, bf16[128,2048]{1,0:T(8,128)(2,1)S(1)} %copy-done.38, f32[128,640]{1,0:T(8,128)S(1)} %copy-done.5, f32[640]{0:T(1024)S(1)} %get-tuple-element.521, f32[128]{0:T(128)S(1)} %copy-done.55), kind=kOutput, calls=%fused_computation.50 | convolution fusion | flops 676052992 | bytes 6622208 | tf_op jit(solution)/shard_map/dot_general | solution.py:597
  293.6 9.0 %reshape.343.refs_2_ = bf16[20480,128]{1,0:T(8,128)(2,1)} reshape(bf16[640,4096]{1,0:T(8,128)(2,1)} %convolution_convert_fusion) | data formatting | bytes 10485760 | tf_op jit(solution)/shard_map/reshape | solution.py:698
  303.5 3.1 reshape.344.refs_3_
  307.5 70.6 %shard_map.180 = (f32[1360,128]{1,0:T(8,128)}, f32[8,128]{1,0:T(8,128)}) custom-call(bf16[7680,128]{1,0:T(8,128)(2,1)} %reshape.341.refs_0_, bf16[5120,128]{1,0:T(8,128)(2,1)} %reshape.342.refs_1_, bf16[20480,128]{1,0:T(8,128)(2,1)} %reshape.343.refs_2_, bf16[10240,128]{1,0:T(8,128)(2,1)} %reshape.344.refs_3_, f32[256,128]{1,0:T(8,128)} %pad_bitcast_fusion.refs_4_), custom_call_target="tpu_custom_call" | custom-call | tf_op jit(solution)/shard_map/pallas_call | solution.py:283
  379.5 2.8 multiply_subtract_fusion
  (310 shorter events, 56.1 us)
Async XLA Ops:
  60.0 18.5 %copy-start.71 = (s32[32]{0:T(128)S(1)}, s32[32]{0:T(128)}, u32[]{:S(2)}) copy-start(s32[32]{0:T(128)} %param.23) | copy-start | bytes 388
  82.4 3.9 %copy-start.10 = (f32[1,128,640]{2,1,0:T(8,128)S(1)}, f32[1,128,640]{2,1,0:T(8,128)}, u32[]{:S(2)}) copy-start(f32[1,128,640]{2,1,0:T(8,128)} %param.20) | copy-start | bytes 983044
  86.9 27.4 %copy-start.8 = (f32[128,1536]{1,0:T(8,128)}, f32[128,1536]{1,0:T(8,128)S(1)}, u32[]{:S(2)}) copy-start(f32[128,1536]{1,0:T(8,128)S(1)} %fusion.57) | copy-start | bytes 2359300
  87.3 22.7 %copy-start.48 = (f32[256]{0:T(256)}, f32[256]{0:T(256)S(1)}, u32[]{:S(2)}) copy-start(f32[256]{0:T(256)S(1)} %get-tuple-element.525) | copy-start | bytes 3076
  87.4 29.3 %copy-start.46 = (f32[256]{0:T(256)}, f32[256]{0:T(256)S(1)}, u32[]{:S(2)}) copy-start(f32[256]{0:T(256)S(1)} %get-tuple-element.524) | copy-start | bytes 3076
  87.5 25.0 %copy-start.65 = (f32[128]{0:T(128)}, f32[128]{0:T(128)S(1)}, u32[]{:S(2)}) copy-start(f32[128]{0:T(128)S(1)} %multiply_reduce_fusion.15) | copy-start | bytes 1540
  87.5 25.0 %copy-start.56 = (f32[128]{0:T(128)}, f32[128]{0:T(128)S(1)}, u32[]{:S(2)}) copy-start(f32[128]{0:T(128)S(1)} %fusion.72) | copy-start | bytes 1540
  87.9 22.2 %copy-start.33 = (f32[128,128]{1,0:T(8,128)}, f32[128,128]{1,0:T(8,128)S(1)}, u32[]{:S(2)}) copy-start(f32[128,128]{1,0:T(8,128)S(1)} %get-tuple-element.526) | copy-start | bytes 196612
  87.9 22.2 %copy-start.35 = (f32[128,128]{1,0:T(8,128)}, f32[128,128]{1,0:T(8,128)S(1)}, u32[]{:S(2)}) copy-start(f32[128,128]{1,0:T(8,128)S(1)} %get-tuple-element.527) | copy-start | bytes 196612
  144.9 19.7 %copy-start.43 = (s32[256]{0:T(256)}, s32[256]{0:T(256)S(1)}, u32[]{:S(2)}) copy-start(s32[256]{0:T(256)S(1)} %get-tuple-element.925) | copy-start | bytes 3076
  145.2 19.4 %copy-start.25 = (bf16[128,1024]{1,0:T(8,128)(2,1)}, bf16[128,1024]{1,0:T(8,128)(2,1)S(1)}, u32[]{:S(2)}) copy-start(bf16[128,1024]{1,0:T(8,128)(2,1)S(1)} %reshape.335) | copy-start | bytes 786436
  166.6 17.0 %copy-start.4 = (f32[128,640]{1,0:T(8,128)}, f32[128,640]{1,0:T(8,128)S(1)}, u32[]{:S(2)}) copy-start(f32[128,640]{1,0:T(8,128)S(1)} %get-tuple-element.488) | copy-start | bytes 983044
  166.6 17.0 %copy-start.54 = (f32[128]{0:T(128)}, f32[128]{0:T(128)S(1)}, u32[]{:S(2)}) copy-start(f32[128]{0:T(128)S(1)} %fusion.74) | copy-start | bytes 1540
  170.6 3.4 copy-start.19
  170.6 2.6 copy-start.14
  174.9 3.2 copy-start.29
  178.1 5.4 %copy-start.37 = (bf16[128,2048]{1,0:T(8,128)(2,1)}, bf16[128,2048]{1,0:T(8,128)(2,1)S(1)}, u32[]{:S(2)}) copy-start(bf16[128,2048]{1,0:T(8,128)(2,1)S(1)} %get-tuple-element.497) | copy-start | bytes 1572868
  178.1 5.4 %copy-start.39 = (bf16[128,2048]{1,0:T(8,128)(2,1)}, bf16[128,2048]{1,0:T(8,128)(2,1)S(1)}, u32[]{:S(2)}) copy-start(bf16[128,2048]{1,0:T(8,128)(2,1)S(1)} %get-tuple-element.498) | copy-start | bytes 1572868
  184.4 5.1 %copy-start.15 = (f32[128,640]{1,0:T(8,128)}, f32[128,640]{1,0:T(8,128)S(1)}, u32[]{:S(2)}) copy-start(f32[128,640]{1,0:T(8,128)S(1)} %get-tuple-element.486) | copy-start | bytes 983044
  185.7 6.2 %copy-start.31 = (bf16[128,640]{1,0:T(8,128)(2,1)}, bf16[128,640]{1,0:T(8,128)(2,1)S(1)}, u32[]{:S(2)}) copy-start(bf16[128,640]{1,0:T(8,128)(2,1)S(1)} %fusion.50) | copy-start | bytes 491524
  189.4 2.5 copy-start.44
  191.9 5.1 %copy-start = (bf16[256,256]{1,0:T(8,128)(2,1)}, bf16[256,256]{1,0:T(8,128)(2,1)S(1)}, u32[]{:S(2)}) copy-start(bf16[256,256]{1,0:T(8,128)(2,1)S(1)} %get-tuple-element.893) | copy-start | bytes 393220 | tf_op jit(solution)/shard_map/while
  191.9 5.2 %copy-start.61 = (f32[256]{0:T(256)}, f32[256]{0:T(256)S(1)}, u32[]{:S(2)}) copy-start(f32[256]{0:T(256)S(1)} %get-tuple-element.894) | copy-start | bytes 3076 | tf_op jit(solution)/shard_map/while
  215.5 5.2 %copy-start = (bf16[256,256]{1,0:T(8,128)(2,1)}, bf16[256,256]{1,0:T(8,128)(2,1)S(1)}, u32[]{:S(2)}) copy-start(bf16[256,256]{1,0:T(8,128)(2,1)S(1)} %get-tuple-element.893) | copy-start | bytes 393220 | tf_op jit(solution)/shard_map/while
  215.5 5.2 %copy-start.61 = (f32[256]{0:T(256)}, f32[256]{0:T(256)S(1)}, u32[]{:S(2)}) copy-start(f32[256]{0:T(256)S(1)} %get-tuple-element.894) | copy-start | bytes 3076 | tf_op jit(solution)/shard_map/while
  222.4 2.6 copy-start.3
  252.2 22.4 %copy-start.36 = (f32[128,128]{1,0:T(8,128)S(1)}, f32[128,128]{1,0:T(8,128)}, u32[]{:S(2)}) copy-start(f32[128,128]{1,0:T(8,128)} %copy-done.35) | copy-start | bytes 196612
  252.2 23.4 %copy-start.9 = (f32[128,1536]{1,0:T(8,128)S(1)}, f32[128,1536]{1,0:T(8,128)}, u32[]{:S(2)}) copy-start(f32[128,1536]{1,0:T(8,128)} %copy-done.8) | copy-start | bytes 2359300
  252.2 23.4 %copy-start.34 = (f32[128,128]{1,0:T(8,128)S(1)}, f32[128,128]{1,0:T(8,128)}, u32[]{:S(2)}) copy-start(f32[128,128]{1,0:T(8,128)} %copy-done.33) | copy-start | bytes 196612
  252.2 23.4 %copy-start.49 = (f32[256]{0:T(256)S(1)}, f32[256]{0:T(256)}, u32[]{:S(2)}) copy-start(f32[256]{0:T(256)} %copy-done.48) | copy-start | bytes 3076
  252.3 23.4 %copy-start.57 = (f32[128]{0:T(128)S(1)}, f32[128]{0:T(128)}, u32[]{:S(2)}) copy-start(f32[128]{0:T(128)} %copy-done.56) | copy-start | bytes 1540
  252.3 24.4 %copy-start.66 = (f32[128]{0:T(128)S(1)}, f32[128]{0:T(128)}, u32[]{:S(2)}) copy-start(f32[128]{0:T(128)} %copy-done.65) | copy-start | bytes 1540
  252.3 24.5 %copy-start.24 = (f32[128,4]{1,0:T(8,128)S(1)}, f32[128,4]{1,0:T(8,128)}, u32[]{:S(2)}) copy-start(f32[128,4]{1,0:T(8,128)} %copy-done.23) | copy-start | bytes 6148
  274.6 3.5 copy-start.41
  283.9 3.3 copy-start.26
  283.9 3.3 copy-start.32
  293.6 9.0 %copy-start.20 = (bf16[128,2048]{1,0:T(8,128)(2,1)S(1)}, bf16[128,2048]{1,0:T(8,128)(2,1)}, u32[]{:S(2)}) copy-start(bf16[128,2048]{1,0:T(8,128)(2,1)} %copy-done.19) | copy-start | bytes 1572868
  293.6 9.0 %copy-start.30 = (bf16[128,640]{1,0:T(8,128)(2,1)S(1)}, bf16[128,640]{1,0:T(8,128)(2,1)}, u32[]{:S(2)}) copy-start(bf16[128,640]{1,0:T(8,128)(2,1)} %copy-done.29) | copy-start | bytes 491524
  303.4 3.2 copy-start.52
  303.4 3.3 copy-start.60
  303.4 3.3 copy-start.53
  307.5 70.7 %copy-start.67 = (f32[96]{0:T(128)S(1)}, f32[96]{0:T(128)}, u32[]{:S(2)}) copy-start(f32[96]{0:T(128)} %param.25) | copy-start | bytes 1156
  307.5 70.7 %copy-start.68 = (f32[96]{0:T(128)S(1)}, f32[96]{0:T(128)}, u32[]{:S(2)}) copy-start(f32[96]{0:T(128)} %param.28) | copy-start | bytes 1156
  307.5 70.7 %copy-start.69 = (f32[96]{0:T(128)S(1)}, f32[96]{0:T(128)}, u32[]{:S(2)}) copy-start(f32[96]{0:T(128)} %param.29) | copy-start | bytes 1156
  307.5 71.9 %copy-start.17 = (f32[174080]{0:T(1024)S(1)}, f32[174080]{0:T(1024)}, u32[]{:S(2)}) copy-start(f32[174080]{0:T(1024)} %param.24) | copy-start | bytes 2088964
  307.5 71.9 %copy-start.27 = (f32[174080]{0:T(1024)S(1)}, f32[174080]{0:T(1024)}, u32[]{:S(2)}) copy-start(f32[174080]{0:T(1024)} %param.26) | copy-start | bytes 2088964
  307.5 71.9 %copy-start.28 = (f32[174080]{0:T(1024)S(1)}, f32[174080]{0:T(1024)}, u32[]{:S(2)}) copy-start(f32[174080]{0:T(1024)} %param.27) | copy-start | bytes 2088964
  379.4 2.8 copy-start.18
  (30 other events, 46.9 us)

commit v3 on v2

--- a/solution.py
+++ b/solution.py
@@ -355,16 +355,16 @@
     return upstream * cosine_table + turned
 
 
-def split_weights(flat_values):
+def split_weights(row_values):
     width_qkv = HEADS * HD + 2 * HD
     first_end = D * width_qkv
     second_end = first_end + HEADS * HD * D
     third_end = second_end + 2 * D * FF
     return (
-        flat_values[:first_end].reshape(D, width_qkv),
-        flat_values[first_end:second_end].reshape(HEADS * HD, D),
-        flat_values[second_end:third_end].reshape(D, 2 * FF),
-        flat_values[third_end:].reshape(FF, D),
+        row_values[: first_end // LANES].reshape(D, width_qkv),
+        row_values[first_end // LANES : second_end // LANES].reshape(HEADS * HD, D),
+        row_values[second_end // LANES : third_end // LANES].reshape(D, 2 * FF),
+        row_values[third_end // LANES :].reshape(FF, D),
     )
 
 
@@ -388,48 +388,142 @@
     return (weights - LEARN_RATE * update, new_first, new_second)
 
 
-def tile_forward(carried, query_rows, query_order, key_rows, value_rows, key_order):
-    row_peak, row_total, row_accum = carried
+def by_head(flat):
+    return jnp.concatenate([flat[:, h * HD : (h + 1) * HD] for h in range(HEADS)], axis=0)
+
+
+def attend_kernel(query_ref, keyval_ref, query_order_ref, key_order_ref, attn_ref, lse_ref, acc, tot):
+    chunk = pl.program_id(0)
+
+    @pl.when(chunk == 0)
+    def _():
+        acc[...] = jnp.zeros_like(acc)
+        tot[...] = jnp.zeros_like(tot)
+
+    keys, values = keyval_ref[:, :HD], keyval_ref[:, HD:]
     scores = lax.dot_general(
-        key_rows, query_rows, (((1,), (1,)), ((), ())), preferred_element_type=jnp.float32
-    )
-    allowed = key_order[:, None] <= query_order[None, :]
-    masked = jnp.where(allowed, scores, -jnp.inf)
-    new_peak = jnp.maximum(row_peak, jnp.max(masked, axis=0))
-    weights = jnp.exp(masked - new_peak[None, :])
-    rescale = jnp.exp(row_peak - new_peak)
-    new_total = row_total * rescale + jnp.sum(weights, axis=0)
-    weights_low = weights.astype(jnp.bfloat16)
-    update = lax.dot_general(
-        weights_low, value_rows, (((0,), (0,)), ((), ())), preferred_element_type=jnp.float32
-    )
-    return (new_peak, new_total, row_accum * rescale[:, None] + update)
-
-
-def tile_backward(
-    query_rows, query_order, grad_rows, log_total, delta_rows, key_rows, value_rows, key_order
+        by_head(query_ref[...]), keys, (((1,), (1,)), ((), ())), preferred_element_type=jnp.float32
+    )
+    weights = jnp.where(key_order_ref[...] <= query_order_ref[...], jnp.exp(scores), 0.0)
+    tot[...] += jnp.sum(weights, axis=1, keepdims=True)
+    acc[...] += jnp.dot(
+        weights.astype(jnp.bfloat16), values, preferred_element_type=jnp.float32
+    )
+
+    @pl.when(chunk == pl.num_programs(0) - 1)
+    def _():
+        rows = attn_ref.shape[0]
+        total = tot[...]
+        result = (acc[...] / total).astype(jnp.bfloat16)
+        for h in range(HEADS):
+            attn_ref[:, h * HD : (h + 1) * HD] = result[h * rows : (h + 1) * rows]
+        lse_ref[...] = jnp.log(total)
+
+
+def attend_back_kernel(
+    query_ref,
+    grad_ref,
+    keyval_ref,
+    query_order_ref,
+    key_order_ref,
+    lse_ref,
+    delta_ref,
+    grad_query_ref,
+    grad_keyval_ref,
+    acc,
 ):
+    chunk = pl.program_id(0)
+
+    @pl.when(chunk == 0)
+    def _():
+        acc[...] = jnp.zeros_like(acc)
+
+    keys, values = keyval_ref[:, :HD], keyval_ref[:, HD:]
+    queries, grads = by_head(query_ref[...]), by_head(grad_ref[...])
     scores = lax.dot_general(
-        key_rows, query_rows, (((1,), (1,)), ((), ())), preferred_element_type=jnp.float32
-    )
-    allowed = key_order[:, None] <= query_order[None, :]
-    probability = jnp.where(allowed, jnp.exp(scores - log_total[None, :]), 0.0)
-    probability_low = probability.astype(jnp.bfloat16)
-    value_part = jnp.dot(probability_low, grad_rows, preferred_element_type=jnp.float32)
-    grad_prob = lax.dot_general(
-        value_rows, grad_rows, (((1,), (1,)), ((), ())), preferred_element_type=jnp.float32
-    )
-    grad_scores = (probability * (grad_prob - delta_rows[None, :])).astype(jnp.bfloat16)
-    query_part = lax.dot_general(
-        grad_scores, key_rows, (((0,), (0,)), ((), ())), preferred_element_type=jnp.float32
-    )
-    key_part = jnp.dot(grad_scores, query_rows, preferred_element_type=jnp.float32)
-    return (query_part, jnp.concatenate([key_part, value_part], axis=1))
-
-
-def add_rows(term_rows, tile_rows, first_row):
-    current = lax.dynamic_slice_in_dim(term_rows, first_row, tile_rows.shape[0], 0)
-    return lax.dynamic_update_slice_in_dim(term_rows, current + tile_rows, first_row, 0)
+        keys, queries, (((1,), (1,)), ((), ())), preferred_element_type=jnp.float32
+    )
+    weights = jnp.where(
+        key_order_ref[...] <= query_order_ref[...], jnp.exp(scores - lse_ref[...]), 0.0
+    )
+    grad_weights = lax.dot_general(
+        values, grads, (((1,), (1,)), ((), ())), preferred_element_type=jnp.float32
+    )
+    grad_scores = (weights * (grad_weights - delta_ref[...])).astype(jnp.bfloat16)
+    grad_keyval_ref[:, :HD] = jnp.dot(
+        grad_scores, queries, preferred_element_type=jnp.float32
+    ).astype(jnp.bfloat16)
+    grad_keyval_ref[:, HD:] = jnp.dot(
+        weights.astype(jnp.bfloat16), grads, preferred_element_type=jnp.float32
+    ).astype(jnp.bfloat16)
+    acc[...] += lax.dot_general(
+        grad_scores, keys, (((0,), (0,)), ((), ())), preferred_element_type=jnp.float32
+    )
+
+    @pl.when(chunk == pl.num_programs(0) - 1)
+    def _():
+        rows = grad_query_ref.shape[0]
+        for h in range(HEADS):
+            grad_query_ref[:, h * HD : (h + 1) * HD] = acc[h * rows : (h + 1) * rows, :]
+
+
+KEY_CHUNK = 1024
+
+
+def fixed(shape):
+    return pl.BlockSpec(shape, lambda i: (0,) * len(shape))
+
+
+def attend(queries, keyval, query_order, key_order):
+    rows, keys = queries.shape[0], keyval.shape[0]
+    return pl.pallas_call(
+        attend_kernel,
+        grid=(keys // KEY_CHUNK,),
+        out_shape=[
+            jax.ShapeDtypeStruct((rows, HEADS * HD), jnp.bfloat16),
+            jax.ShapeDtypeStruct((HEADS * rows, 1), jnp.float32),
+        ],
+        in_specs=[
+            fixed((rows, HEADS * HD)),
+            pl.BlockSpec((KEY_CHUNK, 2 * HD), lambda i: (i, 0)),
+            fixed((HEADS * rows, 1)),
+            pl.BlockSpec((1, KEY_CHUNK), lambda i: (0, i)),
+        ],
+        out_specs=[fixed((rows, HEADS * HD)), fixed((HEADS * rows, 1))],
+        scratch_shapes=[
+            pltpu.VMEM((HEADS * rows, HD), jnp.float32),
+            pltpu.VMEM((HEADS * rows, 1), jnp.float32),
+        ],
+        compiler_params=pltpu.CompilerParams(vmem_limit_bytes=40 << 20),
+    )(queries, keyval, query_order[:, None], key_order[None, :])
+
+
+def attend_back(queries, grads, keyval, query_order, key_order, lse, delta):
+    rows, keys = queries.shape[0], keyval.shape[0]
+    row = fixed((1, HEADS * rows))
+    return pl.pallas_call(
+        attend_back_kernel,
+        grid=(keys // KEY_CHUNK,),
+        out_shape=[
+            jax.ShapeDtypeStruct((rows, HEADS * HD), jnp.float32),
+            jax.ShapeDtypeStruct((keys, 2 * HD), jnp.bfloat16),
+        ],
+        in_specs=[
+            fixed((rows, HEADS * HD)),
+            fixed((rows, HEADS * HD)),
+            pl.BlockSpec((KEY_CHUNK, 2 * HD), lambda i: (i, 0)),
+            row,
+            pl.BlockSpec((KEY_CHUNK, 1), lambda i: (i, 0)),
+            row,
+            row,
+        ],
+        out_specs=[
+            fixed((rows, HEADS * HD)),
+            pl.BlockSpec((KEY_CHUNK, 2 * HD), lambda i: (i, 0)),
+        ],
+        scratch_shapes=[pltpu.VMEM((HEADS * rows, HD), jnp.float32)],
+        compiler_params=pltpu.CompilerParams(vmem_limit_bytes=40 << 20),
+    )(queries, grads, keyval, query_order[None, :], key_order[:, None], lse, delta)
 
 
 def shards(
@@ -468,15 +562,13 @@
         ],
         0,
     )
-    gathered = gathered[:, :shard_rows].reshape(-1)
+    gathered = gathered[:, :shard_rows].reshape(-1, LANES)
     gains_low = gain_rows[:, 0, :gain_count].reshape(-1)
     w_qkv, w_out, w_gateup, w_down = split_weights(gathered)
     gain_in, gain_query, gain_key, gain_attn, gain_ffn, gain_post = split_gains(
         gains_low.astype(jnp.float32)
     )
     token_rows = inputs.shape[1]
-    query_count = token_rows * HEADS
-    upper_span = BLK * HEADS
     query_scale = HD ** (-0.5)
     residual_in = inputs[0]
     grad_output = cotangent[0]
@@ -492,11 +584,9 @@
         ),
         axis=1,
     )
-    lower_block = jnp.min(own_blocks)
-    upper_block = jnp.max(own_blocks)
-    upper_start = jnp.where(own_blocks[1] > own_blocks[0], 1, 0) * upper_span
     token_order = (own_blocks[:, None] * BLK + block_offsets[None, :]).reshape(token_rows)
-    query_order = jnp.repeat(token_order, HEADS)
+    query_order = jnp.tile(token_order, HEADS)
+    key_order = (block_map[:, None] * BLK + block_offsets[None, :]).reshape(num_blocks * BLK)
     cosine_table, sine_table = rope_tables(positions[0])
     normed_in = rms_apply(residual_in, gain_in).astype(jnp.bfloat16)
     projected = jnp.dot(normed_in, w_qkv, preferred_element_type=jnp.float32)
@@ -508,76 +598,16 @@
     query_rows = (
         (rotate(query_normed, cosine_table[:, None], sine_table[:, None]) * query_scale)
         .astype(jnp.bfloat16)
-        .reshape(query_count, HD)
+        .reshape(token_rows, HEADS * HD)
     )
     own_keyval = jnp.concatenate(
         [rotate(key_normed, cosine_table, sine_table), value_raw], axis=1
     ).astype(jnp.bfloat16)
-    upper_queries = lax.dynamic_slice_in_dim(query_rows, upper_start, upper_span, 0)
-    upper_order = lax.dynamic_slice_in_dim(query_order, upper_start, upper_span, 0)
-
-    def group_forward(carried, key_rows, value_rows, key_order, least_block):
-
-        def group_full_rows(inner):
-            return tile_forward(inner, query_rows, query_order, key_rows, value_rows, key_order)
-
-        def group_upper_rows(inner):
-            part_state = tuple(
-                (lax.dynamic_slice_in_dim(member, upper_start, upper_span, 0) for member in inner)
-            )
-            new_state = tile_forward(
-                part_state, upper_queries, upper_order, key_rows, value_rows, key_order
-            )
-            return tuple(
-                (
-                    lax.dynamic_update_slice_in_dim(member, fresh, upper_start, 0)
-                    for member, fresh in zip(inner, new_state)
-                )
-            )
-
-        def group_no_rows(inner):
-            return inner
-
-        branch = jnp.where(
-            least_block <= lower_block, 0, jnp.where(least_block <= upper_block, 1, 2)
-        )
-        return lax.switch(branch, [group_full_rows, group_upper_rows, group_no_rows], carried)
-
-    group_blocks = 16
-    group_count = num_blocks // group_blocks
-    group_keys = group_blocks * BLK
-    group_index = jnp.arange(group_count, dtype=jnp.int32)
-    init_forward = (
-        jnp.full((query_count,), -jnp.inf, jnp.float32),
-        jnp.zeros((query_count,), jnp.float32),
-        jnp.zeros((query_count, HD), jnp.float32),
-    )
     (early_kv, late_kv), (order_c, order_d) = row_parts(token_rows, 8), sequence.orders()
     keyval_parts = ((0,) + early_kv + (order_c,), (0,) + late_kv + (order_d,))
     (all_keyval,) = gather_all(sequence, keyval_parts, [own_keyval], 2)
-    all_keyval = all_keyval.reshape(num_blocks, BLK, 2 * HD)
-    inverse = jnp.sum(
-        jnp.where(block_map[None, :] == block_ids[:, None], block_ids[None, :], 0), axis=1
-    )
-    sorted_keyval = all_keyval[inverse].reshape(group_count, group_keys, 2 * HD)
-    sorted_keys = sorted_keyval[:, :, :HD]
-    sorted_values = sorted_keyval[:, :, HD:]
-
-    def kept_forward(inner, scan_item):
-        key_rows, value_rows, group_id = scan_item
-        key_order = group_id * group_keys + jnp.arange(group_keys, dtype=jnp.int32)
-        return (
-            group_forward(inner, key_rows, value_rows, key_order, group_id * group_blocks),
-            None,
-        )
-
-    forward_state, _ = lax.scan(
-        kept_forward, init_forward, (sorted_keys, sorted_values, group_index)
-    )
-    row_peak, row_total, row_accum = forward_state
-    log_total = row_peak + jnp.log(row_total)
-    attn_rows = lax.optimization_barrier((row_accum / row_total[:, None]).astype(jnp.bfloat16))
-    attn_flat = attn_rows.reshape(token_rows, HEADS * HD)
+    all_keyval = all_keyval.reshape(num_blocks * BLK, 2 * HD)
+    attn_flat, log_total = attend(query_rows, all_keyval, query_order, key_order)
     branch_attn = jnp.dot(attn_flat, w_out, preferred_element_type=jnp.float32)
     after_attn = residual_in + rms_apply(branch_attn, gain_attn)
     normed_mid = rms_apply(after_attn, gain_ffn).astype(jnp.bfloat16)
@@ -601,69 +631,26 @@
     grad_attn_branch, grad_gain_attn = norm_back(branch_attn, gain_attn, grad_after)
     grad_attn_low = grad_attn_branch.astype(jnp.bfloat16)
     grad_wout = jnp.dot(attn_flat.T, grad_attn_low, preferred_element_type=jnp.float32)
-    grad_rows = lax.optimization_barrier(
-        jnp.dot(grad_attn_low, w_out.T, preferred_element_type=jnp.float32).astype(jnp.bfloat16)
-    ).reshape(query_count, HD)
-    delta_rows = jnp.sum(grad_rows.astype(jnp.float32) * attn_rows.astype(jnp.float32), axis=1)
-    upper_grads = lax.dynamic_slice_in_dim(grad_rows, upper_start, upper_span, 0)
-    upper_lse = lax.dynamic_slice_in_dim(log_total, upper_start, upper_span, 0)
-    upper_delta = lax.dynamic_slice_in_dim(delta_rows, upper_start, upper_span, 0)
-
-    def tile_terms(grad_query, key_rows, value_rows, key_order, least_block):
-
-        def tile_full_rows(inner):
-            query_part, tile_rows = tile_backward(
-                query_rows,
-                query_order,
-                grad_rows,
-                log_total,
-                delta_rows,
-                key_rows,
-                value_rows,
-                key_order,
-            )
-            return (inner + query_part, tile_rows)
-
-        def tile_upper_rows(inner):
-            query_part, tile_rows = tile_backward(
-                upper_queries,
-                upper_order,
-                upper_grads,
-                upper_lse,
-                upper_delta,
-                key_rows,
-                value_rows,
-                key_order,
-            )
-            return (add_rows(inner, query_part, upper_start), tile_rows)
-
-        def tile_no_rows(inner):
-            return (inner, jnp.zeros((key_rows.shape[0], 2 * HD), jnp.float32))
-
-        branch = jnp.where(
-            least_block <= lower_block, 0, jnp.where(least_block <= upper_block, 1, 2)
-        )
-        return lax.switch(branch, [tile_full_rows, tile_upper_rows, tile_no_rows], grad_query)
-
-    zero_query = jnp.zeros((query_count, HD), jnp.float32)
-
-    def kept_backward(inner, scan_item):
-        grad_query, term_rows = inner
-        key_rows, value_rows, group_id = scan_item
-        key_order = group_id * group_keys + jnp.arange(group_keys, dtype=jnp.int32)
-        grad_query, tile_rows = tile_terms(
-            grad_query, key_rows, value_rows, key_order, group_id * group_blocks
-        )
-        return ((grad_query, add_rows(term_rows, tile_rows, group_id * group_keys)), None)
-
-    init_backward = (zero_query, jnp.zeros((num_blocks * BLK, 2 * HD), jnp.float32))
-    backward_state, _ = lax.scan(
-        kept_backward, init_backward, (sorted_keys, sorted_values, group_index)
-    )
-    grad_query_all, seq_terms = backward_state
-    slot_terms = seq_terms.astype(jnp.bfloat16).reshape(num_blocks, BLK, 2 * HD)[block_map]
+    grad_rows = jnp.dot(grad_attn_low, w_out.T, preferred_element_type=jnp.float32).astype(
+        jnp.bfloat16
+    )
+    delta_rows = jnp.sum(
+        (grad_rows.astype(jnp.float32) * attn_flat.astype(jnp.float32)).reshape(
+            token_rows, HEADS, HD
+        ),
+        axis=2,
+    )
+    grad_query_all, slot_terms = attend_back(
+        query_rows,
+        grad_rows,
+        all_keyval,
+        query_order,
+        key_order,
+        log_total.reshape(1, HEADS * token_rows),
+        delta_rows.T.reshape(1, HEADS * token_rows),
+    )
     (key_terms,) = reduce_all(
-        sequence, keyval_parts, [[slot_terms.reshape(num_blocks * BLK, 2 * HD)]], 3
+        sequence, keyval_parts, [[slot_terms]], 3
     )
     grad_key_rot = key_terms[:, :HD]
     grad_value = key_terms[:, HD:]

time: 390 us -> 308 us (0.79); the launches traced: 383 us -> 306 us
  local copies, waits for them, and re-layouts: 119 us -> 79.6 us
  loops' own time: 20 us -> 0 us
  matrix products: 36.6 us -> 21.7 us
  other arithmetic: 35.6 us -> 27.6 us
  Pallas kernels: 169 us -> 175 us
    slice x5 -> x4, local copies, waits for them, and re-layouts: 41.9 us -> 13.2 us  [the longest x1 5.74 us: split_weights(): row_values[second_end // LANES:third_end // LANES].reshape(D, 2 * FF)]
    another operation x6 -> x0, loops' own time: 20 us -> none  [the longest x1 14.5 us: shards(): lax.scan(kept_backward, init_backward, (sorted_keys, sorted_values, group...]
    reshape x4 -> x5, local copies, waits for them, and re-layouts: 4.27 us -> 23 us  [the longest x1 8.8 us: split_weights(): row_values[second_end // LANES:third_end // LANES].reshape(D, 2 * FF)]
    dynamic_slice x13 -> x0, local copies, waits for them, and re-layouts: 18.4 us -> none  [the longest x4 12.2 us: add_rows(): lax.dynamic_slice_in_dim(term_rows, first_row, tile_rows.shape[0], 0)]
    dynamic_update_slice x6 -> x0, local copies, waits for them, and re-layouts: 10.6 us -> none  [the longest x5 8.73 us: add_rows(): lax.dynamic_update_slice_in_dim(term_rows, current + tile_rows, first_row...]
    dot_general x14 -> x0, matrix products: 10.6 us -> none  [the longest x2 2 us: tile_forward(): lax.dot_general(weights_low, value_rows, (((0,), (0,)), ((), ())), prefer...]
    unnamed x144 -> x178, local copies, waits for them, and re-layouts: 4.04 us -> 14.6 us
    add x8 -> x1, other arithmetic: 8.09 us -> 0.07 us  [shards(): block_map[:, None] * BLK + block_offsets[None, :]]
where the time goes in v3:
time: 308 us; the launch traced here: 306 us
  Pallas kernels  175 us (57%)
  local copies, waits for them, and re-layouts  79.6 us (26%)
  other arithmetic  27.6 us (9%)
  matrix products  21.7 us (7%)
    pallas_call x2, Pallas kernels, reduce_all(): pl.pallas_call(functools.partial(reduce_kernel, group, parts, [[piece.sha...  92.9 us
    pallas_call x2, Pallas kernels, gather_all(): pl.pallas_call(functools.partial(gather_kernel, group, parts, len(owns)),...  77.1 us
    reshape x4, local copies, waits for them, and re-layouts, shards(): term.astype(jnp.bfloat16).reshape(-1, LANES)  21.2 us
    unnamed x178, local copies, waits for them, and re-layouts  14.6 us
    reshape x1, local copies, waits for them, and re-layouts, split_weights(): row_values[second_end // LANES:third_end // LANES].reshape(D, 2 * FF)  8.8 us

profile of v3, /device:TPU:0, one launch (start us, length us, event | category | flops | bytes accessed | tf_op | source)
XLA Modules:
  0.0 306.1 jit_solution(16231573785067791788)
XLA Ops:
  1.5 1.1 fusion.16
  5.7 1.9 convert_bitcast_fusion.refs_0_
  7.6 1.0 add.269.key_order_ref
  8.6 56.3 %shard_map.177 = (bf16[32,1360,128]{2,1,0:T(8,128)(2,1)}, bf16[32,16,128]{2,1,0:T(8,128)(2,1)}) custom-call(bf16[1360,128]{1,0:T(8,128)(2,1)} %convert_bitcast_fusion.refs_0_, bf16[16,128]{1,0:T(8,128)(2,1)} %pad.8.refs_1_), custom_call_target="tpu_custom_call" | custom-call | tf_op jit(solution)/shard_map/pallas_call | solution.py:155
  67.1 1.4 slice.121
  68.5 1.8 reshape.322
  70.3 3.1 slice.111
  73.3 4.8 %reshape.319 = bf16[640,1536]{1,0:T(8,128)(2,1)} reshape(bf16[7680,128]{1,0:T(8,128)(2,1)} %slice.111) | data formatting | bytes 3932160 | tf_op jit(solution)/shard_map/reshape | solution.py:364
  78.1 2.1 fusion.19
  82.3 0.9 copy.42
  87.1 20.8 %shard_map.178 = bf16[16,128,512]{2,1,0:T(8,128)(2,1)} custom-call(bf16[128,512]{1,0:T(8,128)(2,1)} %pad_maximum_fusion.9.refs_0_), custom_call_target="tpu_custom_call" | custom-call | tf_op jit(solution)/shard_map/pallas_call | solution.py:155
  108.0 1.6 copy-done
  109.6 1.9 shard_map.179
  112.1 1.2 multiply_reduce_fusion.10
  113.4 3.0 slice.127
  116.4 5.7 %slice.124 = bf16[20480,128]{1,0:T(8,128)(2,1)} slice(bf16[43520,128]{1,0:T(8,128)(2,1)} %bitcast.98), slice={[12800:33280], [0:128]} | slice | bytes 10485760 | tf_op jit(solution)/shard_map/slice | solution.py:366
  122.1 8.8 %reshape.323 = bf16[640,4096]{1,0:T(8,128)(2,1)} reshape(bf16[20480,128]{1,0:T(8,128)(2,1)} %slice.124) | data formatting | bytes 10485760 | tf_op jit(solution)/shard_map/reshape | solution.py:366
  130.9 5.6 %reshape.324 = bf16[2048,640]{1,0:T(8,128)(2,1)} reshape(bf16[10240,128]{1,0:T(8,128)(2,1)} %slice.127) | data formatting | bytes 5242880 | tf_op jit(solution)/shard_map/reshape | solution.py:367
  136.5 3.5 %fusion.41 = f32[128,4096]{1,0:T(8,128)S(1)} fusion(bf16[640,4096]{1,0:T(8,128)(2,1)} %reshape.323, f32[128,640]{1,0:T(8,128)S(1)} %get-tuple-element.46, f32[640]{0:T(1024)S(1)} %get-tuple-element.69, f32[128]{0:T(128)S(1)} %fusion.35), kind=kOutput, calls=%fused_computation.152 | convolution fusion | flops 671334400 | bytes 7670784 | tf_op jit(solution)/shard_map/dot_general | solution.py:614
  140.4 1.4 copy-done.14
  144.5 1.4 fusion.6
  146.5 2.4 multiply_reduce_fusion.3
  150.6 1.4 convert_multiply_fusion
  152.0 2.1 reshape.326
  154.1 1.9 reduce_sum.204
  155.9 0.9 copy.36
  156.8 1.0 copy-done.3
  157.8 0.9 copy-done.7
  158.8 3.6 %shard_map.180 = (f32[128,1024]{1,0:T(8,128)S(1)}, bf16[2048,512]{1,0:T(8,128)(2,1)S(1)}) custom-call(bf16[128,1024]{1,0:T(8,128)(2,1)S(1)} %copy-done.3, bf16[128,1024]{1,0:T(8,128)(2,1)S(1)} %copy-done.7, bf16[2048,512]{1,0:T(8,128)(2,1)S(1)} %bitcast.88, s32[1,512]{1,0:T(1,128)S(1)} %bitcast.90, s32[2048,1]{1,0:T(8,128)S(1)} %add.269.key_order_ref, ...), custom_call_target="tpu_custom_call" | custom-call | tf_op jit(solution)/shard_map/pallas_call | solution.py:504
  162.3 1.3 copy-done.4
  164.5 22.3 %shard_map.181 = f32[128,512]{1,0:T(8,128)} custom-call(bf16[2048,512]{1,0:T(8,128)(2,1)} %copy-done.4), custom_call_target="tpu_custom_call" | custom-call | tf_op jit(solution)/shard_map/pallas_call | solution.py:283
  186.8 1.5 slice.174
  188.3 0.9 slice_multiply_fusion
  189.3 1.7 multiply_reduce_fusion.12
  192.4 1.0 pad_maximum_fusion.3
  194.3 0.9 copy.38
  195.7 1.6 multiply_reduce_fusion
  200.7 1.8 reshape.330.refs_1_
  202.6 2.1 convolution_convert_fusion.1
  204.6 4.8 %reshape.329.refs_0_ = bf16[7680,128]{1,0:T(8,128)(2,1)} reshape(bf16[640,1536]{1,0:T(8,128)(2,1)} %convolution_convert_fusion.1) | data formatting | bytes 3932160 | tf_op jit(solution)/shard_map/reshape | solution.py:685
  209.5 2.4 convolution_convert_fusion.2
  211.8 5.6 %reshape.332.refs_3_ = bf16[10240,128]{1,0:T(8,128)(2,1)} reshape(bf16[2048,640]{1,0:T(8,128)(2,1)} %convolution_convert_fusion.2) | data formatting | bytes 5242880 | tf_op jit(solution)/shard_map/reshape | solution.py:685
  217.5 4.0 %convolution_convert_fusion = bf16[640,4096]{1,0:T(8,128)(2,1)} fusion(bf16[128,2048]{1,0:T(8,128)(2,1)S(1)} %copy-done.43, bf16[128,2048]{1,0:T(8,128)(2,1)S(1)} %copy-done.41, f32[128,640]{1,0:T(8,128)S(1)} %copy-done.13, f32[640]{0:T(1024)S(1)} %get-tuple-element.69, f32[128]{0:T(128)S(1)} %copy-done.64), kind=kOutput, calls=%fused_computation | convolution fusion | flops 676052992 | bytes 6622208 | tf_op jit(solution)/shard_map/dot_general | solution.py:627
  221.5 8.9 %reshape.331.refs_2_ = bf16[20480,128]{1,0:T(8,128)(2,1)} reshape(bf16[640,4096]{1,0:T(8,128)(2,1)} %convolution_convert_fusion) | data formatting | bytes 10485760 | tf_op jit(solution)/shard_map/reshape | solution.py:685
  230.5 70.6 %shard_map.182 = (f32[1360,128]{1,0:T(8,128)}, f32[8,128]{1,0:T(8,128)}) custom-call(bf16[7680,128]{1,0:T(8,128)(2,1)} %reshape.329.refs_0_, bf16[5120,128]{1,0:T(8,128)(2,1)} %reshape.330.refs_1_, bf16[20480,128]{1,0:T(8,128)(2,1)} %reshape.331.refs_2_, bf16[10240,128]{1,0:T(8,128)(2,1)} %reshape.332.refs_3_, f32[256,128]{1,0:T(8,128)} %pad_bitcast_fusion.refs_4_), custom_call_target="tpu_custom_call" | custom-call | tf_op jit(solution)/shard_map/pallas_call | solution.py:283
  301.1 1.2 multiply_subtract_fusion.1
  302.4 2.8 multiply_subtract_fusion
  305.2 0.9 copy.54
  (244 shorter events, 24.5 us)
Async XLA Ops:
  2.6 75.5 %copy-start.68 = (f32[128]{0:T(128)}, f32[128]{0:T(128)S(1)}, u32[]{:S(2)}) copy-start(f32[128]{0:T(128)S(1)} %fusion.32) | copy-start | bytes 1540
  65.8 15.0 %copy-start.54 = (f32[256]{0:T(256)}, f32[256]{0:T(256)S(1)}, u32[]{:S(2)}) copy-start(f32[256]{0:T(256)S(1)} %get-tuple-element.72) | copy-start | bytes 3076
  67.1 11.1 %copy-start.48 = (f32[640]{0:T(1024)}, f32[640]{0:T(1024)S(1)}, u32[]{:S(2)}) copy-start(f32[640]{0:T(1024)S(1)} %get-tuple-element.71) | copy-start | bytes 7684
  73.3 4.8 %copy-start.17 = (f32[1,128,640]{2,1,0:T(8,128)S(1)}, f32[1,128,640]{2,1,0:T(8,128)}, u32[]{:S(2)}) copy-start(f32[1,128,640]{2,1,0:T(8,128)} %param.10) | copy-start | bytes 983044
  80.2 5.9 %copy-start.8 = (f32[128,1536]{1,0:T(8,128)}, f32[128,1536]{1,0:T(8,128)S(1)}, u32[]{:S(2)}) copy-start(f32[128,1536]{1,0:T(8,128)S(1)} %fusion.19) | copy-start | bytes 2359300
  80.3 2.9 copy-start.75
  80.3 2.9 copy-start.66
  80.8 3.4 %copy-start.36 = (f32[128,128]{1,0:T(8,128)}, f32[128,128]{1,0:T(8,128)S(1)}, u32[]{:S(2)}) copy-start(f32[128,128]{1,0:T(8,128)S(1)} %get-tuple-element.74) | copy-start | bytes 196612
  80.8 3.4 %copy-start.38 = (f32[128,128]{1,0:T(8,128)}, f32[128,128]{1,0:T(8,128)S(1)}, u32[]{:S(2)}) copy-start(f32[128,128]{1,0:T(8,128)S(1)} %get-tuple-element.75) | copy-start | bytes 196612
  87.1 24.4 %copy-start.2 = (bf16[128,1024]{1,0:T(8,128)(2,1)}, bf16[128,1024]{1,0:T(8,128)(2,1)S(1)}, u32[]{:S(2)}) copy-start(bf16[128,1024]{1,0:T(8,128)(2,1)S(1)} %multiply_convert_fusion.2.query_ref) | copy-start | bytes 786436
  87.1 24.5 %copy-start.10 = (bf16[1024,640]{1,0:T(8,128)(2,1)S(1)}, bf16[1024,640]{1,0:T(8,128)(2,1)}, u32[]{:S(2)}) copy-start(bf16[1024,640]{1,0:T(8,128)(2,1)} %reshape.322) | copy-start | bytes 3932164
  113.3 35.5 %copy-start.12 = (f32[128,640]{1,0:T(8,128)}, f32[128,640]{1,0:T(8,128)S(1)}, u32[]{:S(2)}) copy-start(f32[128,640]{1,0:T(8,128)S(1)} %get-tuple-element.46) | copy-start | bytes 983044
  113.4 35.5 %copy-start.63 = (f32[128]{0:T(128)}, f32[128]{0:T(128)S(1)}, u32[]{:S(2)}) copy-start(f32[128]{0:T(128)S(1)} %fusion.35) | copy-start | bytes 1540
  141.7 2.8 copy-start.20
  143.6 2.4 slice-start
  145.9 2.9 copy-start.40
  145.9 2.9 copy-start.42
  146.5 2.4 copy-start.50
  150.5 6.3 %copy-start.1 = (bf16[16,128,512]{2,1,0:T(8,128)(2,1)S(1)}, bf16[16,128,512]{2,1,0:T(8,128)(2,1)}, u32[]{:S(2)}) copy-start(bf16[16,128,512]{2,1,0:T(8,128)(2,1)} %shard_map.178) | copy-start | bytes 6291460
  164.5 23.9 %copy-start.39 = (f32[128,128]{1,0:T(8,128)S(1)}, f32[128,128]{1,0:T(8,128)}, u32[]{:S(2)}) copy-start(f32[128,128]{1,0:T(8,128)} %copy-done.38) | copy-start | bytes 196612
  164.5 24.8 %copy-start.9 = (f32[128,1536]{1,0:T(8,128)S(1)}, f32[128,1536]{1,0:T(8,128)}, u32[]{:S(2)}) copy-start(f32[128,1536]{1,0:T(8,128)} %copy-done.8) | copy-start | bytes 2359300
  164.5 24.8 %copy-start.37 = (f32[128,128]{1,0:T(8,128)S(1)}, f32[128,128]{1,0:T(8,128)}, u32[]{:S(2)}) copy-start(f32[128,128]{1,0:T(8,128)} %copy-done.36) | copy-start | bytes 196612
  164.5 24.8 %copy-start.55 = (f32[256]{0:T(256)S(1)}, f32[256]{0:T(256)}, u32[]{:S(2)}) copy-start(f32[256]{0:T(256)} %copy-done.54) | copy-start | bytes 3076
  164.5 24.8 %copy-start.67 = (f32[128]{0:T(128)S(1)}, f32[128]{0:T(128)}, u32[]{:S(2)}) copy-start(f32[128]{0:T(128)} %copy-done.66) | copy-start | bytes 1540
  164.5 26.5 %copy-start.76 = (f32[128]{0:T(128)S(1)}, f32[128]{0:T(128)}, u32[]{:S(2)}) copy-start(f32[128]{0:T(128)} %copy-done.75) | copy-start | bytes 1540
  164.5 27.3 %copy-start.6 = (f32[128,1024]{1,0:T(8,128)S(1)}, f32[128,1024]{1,0:T(8,128)}, u32[]{:S(2)}) copy-start(f32[128,1024]{1,0:T(8,128)} %copy-done.5) | copy-start | bytes 1572868
  164.5 27.5 %copy-start.44 = (f32[128,256]{1,0:T(8,128)S(1)}, f32[128,256]{1,0:T(8,128)}, u32[]{:S(2)}) copy-start(f32[128,256]{1,0:T(8,128)} %get-tuple-element.63) | copy-start | bytes 393220
  189.3 3.0 copy-start.16
  189.3 3.0 copy-start.61
  192.2 3.0 copy-start.57
  192.3 3.4 %copy-start.23 = (f32[16,8,4,256]{3,1,2,0:T(8,128)S(1)}, f32[16,8,4,256]{3,1,2,0:T(8,128)}, u32[]{:S(2)}) copy-start(f32[16,8,4,256]{3,1,2,0:T(8,128)} %copy-done.22) | copy-start | bytes 1572868
  193.4 2.3 copy-start.52
  197.5 2.6 copy-start.31
  200.2 2.4 copy-start.47
  200.2 2.4 copy-start.70
  204.6 4.8 %copy-start.21 = (bf16[128,2048]{1,0:T(8,128)(2,1)S(1)}, bf16[128,2048]{1,0:T(8,128)(2,1)}, u32[]{:S(2)}) copy-start(bf16[128,2048]{1,0:T(8,128)(2,1)} %copy-done.20) | copy-start | bytes 1572868
  204.6 4.8 %copy-start.35 = (bf16[128,640]{1,0:T(8,128)(2,1)S(1)}, bf16[128,640]{1,0:T(8,128)(2,1)}, u32[]{:S(2)}) copy-start(bf16[128,640]{1,0:T(8,128)(2,1)} %copy-done.34) | copy-start | bytes 491524
  211.8 5.6 %copy-start.13 = (f32[128,640]{1,0:T(8,128)S(1)}, f32[128,640]{1,0:T(8,128)}, u32[]{:S(2)}) copy-start(f32[128,640]{1,0:T(8,128)} %copy-done.12) | copy-start | bytes 983044
  211.8 5.6 %copy-start.41 = (bf16[128,2048]{1,0:T(8,128)(2,1)S(1)}, bf16[128,2048]{1,0:T(8,128)(2,1)}, u32[]{:S(2)}) copy-start(bf16[128,2048]{1,0:T(8,128)(2,1)} %copy-done.40) | copy-start | bytes 1572868
  211.8 5.6 %copy-start.43 = (bf16[128,2048]{1,0:T(8,128)(2,1)S(1)}, bf16[128,2048]{1,0:T(8,128)(2,1)}, u32[]{:S(2)}) copy-start(bf16[128,2048]{1,0:T(8,128)(2,1)} %copy-done.42) | copy-start | bytes 1572868
  211.8 5.6 %copy-start.64 = (f32[128]{0:T(128)S(1)}, f32[128]{0:T(128)}, u32[]{:S(2)}) copy-start(f32[128]{0:T(128)} %copy-done.63) | copy-start | bytes 1540
  230.4 70.7 %copy-start.77 = (f32[96]{0:T(128)S(1)}, f32[96]{0:T(128)}, u32[]{:S(2)}) copy-start(f32[96]{0:T(128)} %param.15) | copy-start | bytes 1156
  230.4 70.7 %copy-start.78 = (f32[96]{0:T(128)S(1)}, f32[96]{0:T(128)}, u32[]{:S(2)}) copy-start(f32[96]{0:T(128)} %param.18) | copy-start | bytes 1156
  230.4 70.7 %copy-start.79 = (f32[96]{0:T(128)S(1)}, f32[96]{0:T(128)}, u32[]{:S(2)}) copy-start(f32[96]{0:T(128)} %param.19) | copy-start | bytes 1156
  230.4 71.9 %copy-start.27 = (f32[174080]{0:T(1024)S(1)}, f32[174080]{0:T(1024)}, u32[]{:S(2)}) copy-start(f32[174080]{0:T(1024)} %param.14) | copy-start | bytes 2088964
  230.4 71.9 %copy-start.32 = (f32[174080]{0:T(1024)S(1)}, f32[174080]{0:T(1024)}, u32[]{:S(2)}) copy-start(f32[174080]{0:T(1024)} %param.16) | copy-start | bytes 2088964
  230.4 71.9 %copy-start.33 = (f32[174080]{0:T(1024)S(1)}, f32[174080]{0:T(1024)}, u32[]{:S(2)}) copy-start(f32[174080]{0:T(1024)} %param.17) | copy-start | bytes 2088964
  302.4 2.8 copy-start.28
  (34 other events, 46.2 us)
